TPU v7x, 32 devices: a whole 2x2x4 slice. The times are simulated.
32 devices in a mesh: sample: 2 (over y), gx: 16 (over z, x, core).
Axes of the slice: x: 2, y: 2, z: 4, core: 2. Of those that a mesh axis runs over, the one named last changes fastest.
Arguments:
- populations: float32 [19, 32, 128, 256], P(None, ('sample', 'gx')), parts along dimension 1, may hold values from 0.5 to 1.5
- solid_mask: int32 [32, 128, 256], P(('sample', 'gx')), parts along dimension 0, may hold values from 0 to 1, as said below
- relax_rates: float32 [19], replicated, may hold values from 0.7 to 1.9
- body_force: float32 [3], replicated, may hold values from -0.1 to 0.1
Outputs:
- final_populations: float32 [19, 32, 128, 256], P(None, ('sample', 'gx')), parts along dimension 1
There are 2 independent parts, one for each index of `sample`. A program takes and returns all parts, laid end to end along the dimension named above; an argument that names none is the same for every part. Nothing has to cross between parts.
Inputs may be any that keep to these rules, and one draw needn't show every extreme that they name: `solid_mask`: 1 marks a solid node, 0 a fluid node.
All inputs are finite; a program needn't handle non-finite values.
Results may differ from a plain program's by a relative error of at most 0.0003.
Values sent between devices are 32-bit elements; how exact they have to be, the bound alone decides.
No kernel may reach another device: no remote copies, remote signals or barrier semaphores. Data moves between devices by JAX's collectives and lax.ppermute only.
A program may use at most 192 MiB of HBM per device.

v0:
```python
import functools

import jax
import jax.numpy as jnp
import numpy as np
from jax import lax
from jax.experimental import pallas as pl
from jax.experimental.pallas import tpu as pltpu
from jax.sharding import PartitionSpec as P

PIECES = 8
LANES = 128
ROWS = 8

UP = (1, 7, 9, 11, 13)
DOWN = (2, 10, 8, 14, 12)
GROUP_SHIFTS = ((0, 0), (1, 0), (-1, 0), (0, 1), (0, -1))
BOUNCE = (0, 2, 1, 4, 3)
FLAT = (0, 3, 4, 5, 6, 15, 16, 17, 18)
FLAT_SHIFTS = ((0, 0), (1, 0), (-1, 0), (0, 1), (0, -1), (1, 1), (-1, -1), (1, -1), (-1, 1))
FLAT_OPPOSITE = (0, 2, 1, 4, 3, 6, 5, 8, 7)


def moment_tables():
    velocities = np.array(
        [
            [0, 0, 0],
            [1, 0, 0],
            [-1, 0, 0],
            [0, 1, 0],
            [0, -1, 0],
            [0, 0, 1],
            [0, 0, -1],
            [1, 1, 0],
            [-1, -1, 0],
            [1, -1, 0],
            [-1, 1, 0],
            [1, 0, 1],
            [-1, 0, -1],
            [1, 0, -1],
            [-1, 0, 1],
            [0, 1, 1],
            [0, -1, -1],
            [0, 1, -1],
            [0, -1, 1],
        ]
    )
    x, y, z = velocities.T
    polynomials = np.stack(
        [
            np.ones(19),
            x,
            y,
            z,
            x * y,
            x * z,
            y * z,
            x**2,
            y**2,
            z**2,
            x * y**2,
            x * z**2,
            x**2 * y,
            x**2 * z,
            y * z**2,
            y**2 * z,
            x**2 * y**2,
            x**2 * z**2,
            y**2 * z**2,
        ]
    ).astype(np.float64)
    basis = []
    for row in polynomials:
        vector = row.copy()
        for earlier in basis:
            vector = vector - vector @ earlier / (earlier @ earlier) * earlier
        basis.append(vector)
    moments = np.stack(basis)
    classes = ((0, 7, 8, 9, 16, 17, 18), (1, 10, 11), (2, 12, 14), (3, 13, 15))
    tables = []
    for numbers in classes:
        rows = list(numbers)
        lower = moments[rows] @ np.linalg.pinv(polynomials[rows])
        lower = np.where(np.abs(lower) < 1e-12, 0.0, lower)
        inverse = np.linalg.inv(lower)
        inverse = np.where(np.abs(inverse) < 1e-12, 0.0, inverse)
        tables.append((numbers, lower, inverse))
    return tables


def relaxing_entries(rates):
    matrices = []
    for numbers, lower, inverse in moment_tables():
        size = len(numbers)
        matrix = {}
        for i in range(size):
            for j in range(i + 1):
                total = None
                for m in range(j, i + 1):
                    factor = float(inverse[i, m] * lower[m, j])
                    if factor == 0.0:
                        continue
                    term = rates[numbers[m]] * factor
                    total = term if total is None else total + term
                if total is not None:
                    matrix[i, j] = total
        matrices.append(matrix)
    return matrices


def apply_lower(matrix, vector):
    out = []
    for i in range(len(vector)):
        total = None
        for j in range(i + 1):
            if (i, j) in matrix:
                term = matrix[i, j] * vector[j]
                total = term if total is None else total + term
        out.append(total)
    return out


def relax(ahead, back, flat, solid, matrices, cross_rates, push):
    axis_sum = (ahead[0] + back[0], flat[1] + flat[2], flat[3] + flat[4])
    axis_odd = (ahead[0] - back[0], flat[1] - flat[2], flat[3] - flat[4])

    def butterfly(pp, pm, mp, mm):
        a, b, c, d = pp + pm, pp - pm, mp + mm, mp - mm
        return a + c, a - c, b + d, b - d

    xy, xy_x, xy_y, xy_xy = butterfly(ahead[1], ahead[2], back[1], back[2])
    xz, xz_x, xz_z, xz_xz = butterfly(ahead[3], ahead[4], back[3], back[4])
    yz, yz_y, yz_z, yz_yz = butterfly(flat[5], flat[7], flat[8], flat[6])
    sx, sy, sz = axis_sum
    density = (flat[0] + (sx + sy)) + ((sz + xy) + (xz + yz))
    jx = axis_odd[0] + (xy_x + xz_x)
    jy = axis_odd[1] + (xy_y + yz_y)
    jz = axis_odd[2] + (xz_z + yz_z)
    over = 1.0 / density
    ux, uy, uz = jx * over, jy * over, jz * over
    qxx, qyy, qzz = jx * ux, jy * uy, jz * uz
    base = (density - 1.5 * (qxx + (qyy + qzz))) * (1.0 / 9.0)
    hx, hy, hz = 0.5 * qxx, 0.5 * qyy, 0.5 * qzz
    bx, by, bz = base + hx, base + hy, base + hz
    rest = flat[0] - 3.0 * base
    sx, sy, sz = sx - bx, sy - by, sz - bz
    xy, xz, yz = xy - (bx + hy), xz - (bx + hz), yz - (by + hz)
    third = 1.0 / 3.0
    tx, ty, tz = jx * third, jy * third, jz * third
    raw = [
        (rest + (sx + sy)) + ((sz + xy) + (xz + yz)),
        sx + (xy + xz),
        sy + (xy + yz),
        sz + (xz + yz),
        xy,
        xz,
        yz,
    ]
    change = apply_lower(matrices[0], raw)
    total, mx, my, mz, cxy, cxz, cyz = change
    even_xy, even_xz, even_yz = 0.25 * cxy, 0.25 * cxz, 0.25 * cyz
    even_x = 0.5 * (mx - (cxy + cxz))
    even_y = 0.5 * (my - (cxy + cyz))
    even_z = 0.5 * (mz - (cxz + cyz))
    even_rest = (total - (mx + my)) + ((cxy + cxz) + (cyz - mz))

    def odd_class(matrix, along, first, second, mean, force):
        first, second = first - mean, second - mean
        along = along - mean
        change = apply_lower(matrix, [along + (first + second), first, second])
        lift = density * force
        return (
            0.5 * ((change[0] - (change[1] + change[2])) - lift),
            0.25 * (change[1] - lift),
            0.25 * (change[2] - lift),
        )

    odd_x, odd_xy_x, odd_xz_x = odd_class(matrices[1], axis_odd[0], xy_x, xz_x, tx, push[0])
    odd_y, odd_xy_y, odd_yz_y = odd_class(matrices[2], axis_odd[1], xy_y, yz_y, ty, push[1])
    odd_z, odd_xz_z, odd_yz_z = odd_class(matrices[3], axis_odd[2], xz_z, yz_z, tz, push[2])
    both_xy = (xy_xy - jx * uy) * cross_rates[0]
    both_xz = (xz_xz - jx * uz) * cross_rates[1]
    both_yz = (yz_yz - jy * uz) * cross_rates[2]

    def spread(even, first, second, both):
        a, b, c, d = even + first, second + both, even - first, second - both
        return a + b, a - b, c + d, c - d

    xy_pp, xy_pm, xy_mp, xy_mm = spread(even_xy, odd_xy_x, odd_xy_y, both_xy)
    xz_pp, xz_pm, xz_mp, xz_mm = spread(even_xz, odd_xz_x, odd_xz_z, both_xz)
    yz_pp, yz_pm, yz_mp, yz_mm = spread(even_yz, odd_yz_y, odd_yz_z, both_yz)
    new_ahead = [even_x + odd_x, xy_pp, xy_pm, xz_pp, xz_pm]
    new_back = [even_x - odd_x, xy_mp, xy_mm, xz_mp, xz_mm]
    new_flat = [
        even_rest,
        even_y + odd_y,
        even_y - odd_y,
        even_z + odd_z,
        even_z - odd_z,
        yz_pp,
        yz_mm,
        yz_pm,
        yz_mp,
    ]
    out_ahead = [
        jnp.where(solid, back[BOUNCE[k]], ahead[k] - new_ahead[k]) for k in range(5)
    ]
    out_back = [jnp.where(solid, ahead[BOUNCE[k]], back[k] - new_back[k]) for k in range(5)]
    out_flat = [
        jnp.where(solid, flat[FLAT_OPPOSITE[k]], flat[k] - new_flat[k]) for k in range(9)
    ]
    return out_ahead, out_back, out_flat


def local_frame():
    return lax.rem(lax.axis_index("gx"), 2)


def select_channel(side, k):
    return jnp.where(side == 1, UP[k], DOWN[k])


def scalars(rates_ref, force_ref, side):
    rates = [rates_ref[m] for m in range(19)]
    third = 1.0 / 3.0
    sign = jnp.where(side == 1, third, -third).astype(jnp.float32)
    push = (force_ref[0] * sign, force_ref[1] * third, force_ref[2] * third)
    scale = 0.25
    cross = tuple(rates[m] * scale for m in (4, 5, 6))
    return relaxing_entries(rates), cross, push


def shifted(ref, channel, shift):
    value = ref[channel]
    if shift[0]:
        value = pltpu.roll(value, shift[0] % value.shape[0], 0)
    if shift[1]:
        value = pltpu.roll(value, shift[1] % value.shape[1], 1)
    return value


def collide_tiles(load, solid_ref, store, first_row, rows, coefficients):
    matrices, cross, push = coefficients

    def body(t, carry):
        row = pl.multiple_of(first_row + t * ROWS, ROWS)
        for lane in range(0, solid_ref.shape[1], LANES):
            where = (pl.ds(row, ROWS), pl.ds(lane, LANES))
            ahead, back, flat = load(where)
            solid = solid_ref[where] == 1
            store(where, *relax(ahead, back, flat, solid, matrices, cross, push))
        return carry

    lax.fori_loop(0, rows // ROWS, body, 0)


def first_kernel(f_ref, mask_ref, rates_ref, force_ref, off_ref, on_ref, flat_ref, f, solid, out, sems):
    height = solid.shape[0]
    rows = height // PIECES
    copies = []
    for piece in range(PIECES):
        part = pl.ds(piece * rows, rows)
        copies.append(
            (
                pltpu.make_async_copy(f_ref.at[:, part, :], f.at[:, part, :], sems.at[0, piece]),
                pltpu.make_async_copy(mask_ref.at[part, :], solid.at[part, :], sems.at[1, piece]),
            )
        )
        for copy in copies[-1]:
            copy.start()
    side = local_frame()
    coefficients = scalars(rates_ref, force_ref, side)
    toward = [select_channel(side, k) for k in range(5)]
    away = [select_channel(1 - side, k) for k in range(5)]

    def load(where):
        return (
            [f[(toward[k], *where)] for k in range(5)],
            [f[(away[k], *where)] for k in range(5)],
            [f[(FLAT[k], *where)] for k in range(9)],
        )

    def store(where, ahead, back, flat):
        for k, value in enumerate(ahead + back + flat):
            out[(k, *where)] = value

    for piece in range(PIECES):
        for copy in copies[piece]:
            copy.wait()
        collide_tiles(load, solid, store, piece * rows, rows, coefficients)
    finish(out, off_ref, on_ref, flat_ref)


def finish(out, off_ref, on_ref, flat_ref):
    for k in range(5):
        off_ref[k] = shifted(out, k, GROUP_SHIFTS[k])
    for k in range(5):
        on_ref[k] = shifted(out, 5 + k, GROUP_SHIFTS[k])
    for k in range(9):
        flat_ref[k] = shifted(out, 10 + k, FLAT_SHIFTS[k])


def second_kernel(
    off_in, on_in, flat_in, mask_ref, rates_ref, force_ref, off_ref, on_ref, out_ref, solid, out, moved, sems
):
    copy = pltpu.make_async_copy(mask_ref, solid, sems.at[0])
    copy.start()
    side = local_frame()
    coefficients = scalars(rates_ref, force_ref, side)

    def load(where):
        return (
            [on_in[(k, *where)] for k in range(5)],
            [off_in[(k, *where)] for k in range(5)],
            [flat_in[(k, *where)] for k in range(9)],
        )

    def store(where, ahead, back, flat):
        for k, value in enumerate(ahead + back + flat):
            out[(k, *where)] = value

    copy.wait()
    collide_tiles(load, solid, store, 0, solid.shape[0], coefficients)
    finish(out, off_ref, on_ref, moved)
    copies = [
        pltpu.make_async_copy(moved.at[k], out_ref.at[FLAT[k]], sems.at[1 + k]) for k in range(9)
    ]
    for copy in copies:
        copy.start()
    for copy in copies:
        copy.wait()


def place_kernel(own, group_ref, out_in, out_ref, sems):
    del out_in
    side = local_frame()
    side = 1 - side if own else side
    copies = [
        pltpu.make_async_copy(group_ref.at[k], out_ref.at[select_channel(side, k)], sems.at[k])
        for k in range(5)
    ]
    for copy in copies:
        copy.start()
    for copy in copies:
        copy.wait()


def in_vmem(array):
    return pltpu.with_memory_space_constraint(array, pltpu.VMEM)


def in_hbm(array):
    return pltpu.with_memory_space_constraint(array, pltpu.HBM)


def vmem_result(shape):
    return pltpu.VMEM(shape, jnp.float32)


def hbm_result(shape):
    return pltpu.HBM(shape, jnp.float32)


def params(mebibytes):
    return pltpu.CompilerParams(vmem_limit_bytes=mebibytes << 20)


def on_device(populations, solid_mask, relax_rates, body_force):
    channels, depth, height, breadth = populations.shape
    assert depth == 1
    count = lax.axis_size("gx")
    assert count % 2 == 0
    off_pairs = [(i, (i + 1) % count if i % 2 else (i - 1) % count) for i in range(count)]
    on_pairs = [(i, i ^ 1) for i in range(count)]
    plane = in_hbm(populations.reshape(channels, height, breadth))
    mask = in_hbm(solid_mask.reshape(height, breadth))
    relax_rates, body_force = in_hbm(relax_rates), in_hbm(body_force)
    f32 = jnp.float32
    group = vmem_result((5, height, breadth))
    whole = hbm_result((channels, height, breadth))
    anywhere = pl.BlockSpec(memory_space=pl.ANY)
    local = pl.BlockSpec(memory_space=pltpu.VMEM)
    small = pl.BlockSpec(memory_space=pltpu.SMEM)
    sheet = pltpu.VMEM((height, breadth), jnp.int32)
    nodes = height * breadth
    off, on, flat = pl.pallas_call(
        first_kernel,
        out_shape=(group, group, vmem_result((9, height, breadth))),
        in_specs=[anywhere, anywhere, small, small],
        out_specs=(local, local, local),
        scratch_shapes=[
            pltpu.VMEM((channels, height, breadth), f32),
            sheet,
            pltpu.VMEM((channels, height, breadth), f32),
            pltpu.SemaphoreType.DMA((2, PIECES)),
        ],
        cost_estimate=pl.CostEstimate(
            flops=320 * nodes, bytes_accessed=80 * nodes, transcendentals=0
        ),
        compiler_params=params(14),
        name="first_step",
    )(plane, mask, relax_rates, body_force)
    off = lax.ppermute(off, "gx", off_pairs)
    on = lax.ppermute(on, "gx", on_pairs)
    off, on, result = pl.pallas_call(
        second_kernel,
        out_shape=(group, group, whole),
        in_specs=[local, local, local, anywhere, small, small],
        out_specs=(local, local, anywhere),
        scratch_shapes=[
            sheet,
            pltpu.VMEM((channels, height, breadth), f32),
            pltpu.VMEM((9, height, breadth), f32),
            pltpu.SemaphoreType.DMA((10,)),
        ],
        cost_estimate=pl.CostEstimate(
            flops=320 * nodes, bytes_accessed=80 * nodes, transcendentals=0
        ),
        compiler_params=params(14),
        name="second_step",
    )(in_vmem(off), in_vmem(on), flat, mask, relax_rates, body_force)
    off = lax.ppermute(off, "gx", off_pairs)
    on = lax.ppermute(on, "gx", on_pairs)
    for own, arrived in ((False, on), (True, off)):
        result = pl.pallas_call(
            functools.partial(place_kernel, own),
            out_shape=whole,
            in_specs=[local, anywhere],
            out_specs=anywhere,
            scratch_shapes=[pltpu.SemaphoreType.DMA((5,))],
            input_output_aliases={1: 0},
            cost_estimate=pl.CostEstimate(flops=0, bytes_accessed=20 * nodes, transcendentals=0),
            compiler_params=params(4),
        )(in_vmem(arrived), result)
    return result.reshape(channels, depth, height, breadth)


def solution(mesh):
    in_specs = (P(None, ("sample", "gx"), None, None), P(("sample", "gx"), None, None), P(), P())
    out_specs = P(None, ("sample", "gx"), None, None)
    return jax.shard_map(
        on_device, mesh=mesh, in_specs=in_specs, out_specs=out_specs, check_vma=False
    )
```

profile of v0, /device:TPU:1, one launch (start us, length us, event | category | flops | bytes accessed | tf_op | source)
XLA Modules:
  0.0 44.7 jit_solution(12064469776610486945)
XLA Ops:
  0.0 3.8 %first_step.1 = (f32[5,128,256]{2,1,0:T(8,128)S(1)}, f32[5,128,256]{2,1,0:T(8,128)S(1)}, f32[9,128,256]{2,1,0:T(8,128)S(1)}) custom-call(f32[19,128,256]{2,1,0:T(8,128)} %bitcast.5, s32[128,256]{1,0:T(8,128)} %bitcast.6, f32[19]{0:T(128)} %rates_ref.3, f32[3]{0:T(128)} %force_ref.3), custom_call_target="tpu_custom_call" | custom-call | flops 10485760 | bytes 2621440 | tf_op jit(solution)/shard_map/first_step/pallas_call | solution.py:386
  3.8 2.7 %collective-permute-start = (f32[5,128,256]{2,1,0:T(8,128)S(1)}, f32[5,128,256]{2,1,0:T(8,128)S(1)}, u32[]{:S(2)}, u32[]{:S(2)}) collective-permute-start(f32[5,128,256]{2,1,0:T(8,128)S(1)} %get-tuple-element.11), channel_id=1, source_target_pairs={{0,15},{1,2},{2,1},{3,4},{4,3},{5,6},{6,5},{7,8},{8,7},{9,10},{10,... | collective-permute-start | bytes 1966088 | tf_op jit(solution)/shard_map/ppermute | solution.py:403
  6.4 2.9 %collective-permute-start.1 = (f32[5,128,256]{2,1,0:T(8,128)S(1)}, f32[5,128,256]{2,1,0:T(8,128)S(1)}, u32[]{:S(2)}, u32[]{:S(2)}) collective-permute-start(f32[5,128,256]{2,1,0:T(8,128)S(1)} %get-tuple-element.12), channel_id=1, source_target_pairs={{0,1},{1,0},{2,3},{3,2},{4,5},{5,4},{6,7},{7,6},{8,9},{9,8},{10,11... | collective-permute-start | bytes 1966088 | tf_op jit(solution)/shard_map/ppermute | solution.py:404
  9.3 12.4 %collective-permute-done.off_in = f32[5,128,256]{2,1,0:T(8,128)S(1)} collective-permute-done((f32[5,128,256]{2,1,0:T(8,128)S(1)}, f32[5,128,256]{2,1,0:T(8,128)S(1)}, u32[]{:S(2)}, u32[]{:S(2)}) %collective-permute-start) | collective-permute-done | bytes 655392 | tf_op jit(solution)/shard_map/ppermute | solution.py:403
  21.7 0.0 collective-permute-done.1.on_in
  21.7 4.9 %second_step.1 = (f32[5,128,256]{2,1,0:T(8,128)S(1)}, f32[5,128,256]{2,1,0:T(8,128)S(1)}, f32[19,128,256]{2,1,0:T(8,128)}) custom-call(f32[5,128,256]{2,1,0:T(8,128)S(1)} %collective-permute-done.off_in, f32[5,128,256]{2,1,0:T(8,128)S(1)} %collective-permute-done.1.on_in, f32[9,128,256]{2,1,0:T(8,128)S(1)} %get-tuple-element.13.flat_in, s32[128,256]{1,0:T(8,128)} %bitcast.7, ...), custom_call_target="tpu_custom_call" | custom-call | flops 10485760 | bytes 2621440 | tf_op jit(solution)/shard_map/second_step/pallas_call | solution.py:405
  26.6 0.1 collective-permute-start.3
  26.7 1.8 %collective-permute-start.2 = (f32[5,128,256]{2,1,0:T(8,128)S(1)}, f32[5,128,256]{2,1,0:T(8,128)S(1)}, u32[]{:S(2)}, u32[]{:S(2)}) collective-permute-start(f32[5,128,256]{2,1,0:T(8,128)S(1)} %get-tuple-element.14), channel_id=1, source_target_pairs={{0,15},{1,2},{2,1},{3,4},{4,3},{5,6},{6,5},{7,8},{8,7},{9,10},{10,... | collective-permute-start | bytes 1966088 | tf_op jit(solution)/shard_map/ppermute | solution.py:422
  28.5 0.3 collective-permute-done.3.group_ref
  28.8 0.9 %shard_map.46.out_in = f32[19,128,256]{2,1,0:T(8,128)} custom-call(f32[5,128,256]{2,1,0:T(8,128)S(1)} %collective-permute-done.3.group_ref, f32[19,128,256]{2,1,0:T(8,128)} %get-tuple-element.16.out_in), custom_call_target="tpu_custom_call", output_to_operand_aliasing={{}: (1, {})} | custom-call | bytes 655360 | tf_op jit(solution)/shard_map/pallas_call | solution.py:425
  29.7 14.1 %collective-permute-done.2.group_ref = f32[5,128,256]{2,1,0:T(8,128)S(1)} collective-permute-done((f32[5,128,256]{2,1,0:T(8,128)S(1)}, f32[5,128,256]{2,1,0:T(8,128)S(1)}, u32[]{:S(2)}, u32[]{:S(2)}) %collective-permute-start.2) | collective-permute-done | bytes 655392 | tf_op jit(solution)/shard_map/ppermute | solution.py:422
  43.8 0.9 %shard_map.47 = f32[19,128,256]{2,1,0:T(8,128)} custom-call(f32[5,128,256]{2,1,0:T(8,128)S(1)} %collective-permute-done.2.group_ref, f32[19,128,256]{2,1,0:T(8,128)} %shard_map.46.out_in), custom_call_target="tpu_custom_call", output_to_operand_aliasing={{}: (1, {})} | custom-call | bytes 655360 | tf_op jit(solution)/shard_map/pallas_call | solution.py:425
Async XLA Ops:
  3.8 17.9 %collective-permute-start = (f32[5,128,256]{2,1,0:T(8,128)S(1)}, f32[5,128,256]{2,1,0:T(8,128)S(1)}, u32[]{:S(2)}, u32[]{:S(2)}) collective-permute-start(f32[5,128,256]{2,1,0:T(8,128)S(1)} %get-tuple-element.11), channel_id=1, source_target_pairs={{0,15},{1,2},{2,1},{3,4},{4,3},{5,6},{6,5},{7,8},{8,7},{9,10},{10,... | collective-permute-start | bytes 1966088 | tf_op jit(solution)/shard_map/ppermute | solution.py:403
  6.4 15.3 %collective-permute-start.1 = (f32[5,128,256]{2,1,0:T(8,128)S(1)}, f32[5,128,256]{2,1,0:T(8,128)S(1)}, u32[]{:S(2)}, u32[]{:S(2)}) collective-permute-start(f32[5,128,256]{2,1,0:T(8,128)S(1)} %get-tuple-element.12), channel_id=1, source_target_pairs={{0,1},{1,0},{2,3},{3,2},{4,5},{5,4},{6,7},{7,6},{8,9},{9,8},{10,11... | collective-permute-start | bytes 1966088 | tf_op jit(solution)/shard_map/ppermute | solution.py:404
  26.6 2.2 %collective-permute-start.3 = (f32[5,128,256]{2,1,0:T(8,128)S(1)}, f32[5,128,256]{2,1,0:T(8,128)S(1)}, u32[]{:S(2)}, u32[]{:S(2)}) collective-permute-start(f32[5,128,256]{2,1,0:T(8,128)S(1)} %get-tuple-element.15), channel_id=1, source_target_pairs={{0,1},{1,0},{2,3},{3,2},{4,5},{5,4},{6,7},{7,6},{8,9},{9,8},{10,11... | collective-permute-start | bytes 1966088 | tf_op jit(solution)/shard_map/ppermute | solution.py:423
  26.7 17.1 %collective-permute-start.2 = (f32[5,128,256]{2,1,0:T(8,128)S(1)}, f32[5,128,256]{2,1,0:T(8,128)S(1)}, u32[]{:S(2)}, u32[]{:S(2)}) collective-permute-start(f32[5,128,256]{2,1,0:T(8,128)S(1)} %get-tuple-element.14), channel_id=1, source_target_pairs={{0,15},{1,2},{2,1},{3,4},{4,3},{5,6},{6,5},{7,8},{8,7},{9,10},{10,... | collective-permute-start | bytes 1966088 | tf_op jit(solution)/shard_map/ppermute | solution.py:422
where the time goes:
time: 44.8 us; the launch traced here: 44.7 us
  waiting for transfers between devices  26.8 us (60%)
  Pallas kernels  10.4 us (23%)
  starting transfers between devices  7.4 us (17%)
    ppermute x2, waiting for transfers between devices, on_device(): off = lax.ppermute(off, 'gx', off_pairs)  26.6 us
    pallas_call x1, Pallas kernels, on_device(): pl.pallas_call(second_kernel, out_shape=(group, group, whole), in_specs=[...  4.87 us
    ppermute x2, starting transfers between devices, on_device(): off = lax.ppermute(off, 'gx', off_pairs)  4.46 us
    pallas_call x1, Pallas kernels, on_device(): pl.pallas_call(first_kernel, out_shape=(group, group, vmem_result((9, hei...  3.77 us
    ppermute x2, starting transfers between devices, on_device(): on = lax.ppermute(on, 'gx', on_pairs)  2.94 us
    pallas_call x2, Pallas kernels, on_device(): pl.pallas_call(functools.partial(place_kernel, own), out_shape=whole, in_...  1.74 us
  transfers between devices with their start and end apart: 4, of which 3 were waited for; matrix products, arithmetic and copies ran while one was open for 0% of the time, Pallas kernels for 2%

commit v1 on v0

--- a/solution.py
+++ b/solution.py
@@ -8,7 +8,7 @@
 from jax.experimental.pallas import tpu as pltpu
 from jax.sharding import PartitionSpec as P
 
-PIECES = 8
+PARTS = 2
 LANES = 128
 ROWS = 8
 
@@ -230,119 +230,161 @@
     return relaxing_entries(rates), cross, push
 
 
-def shifted(ref, channel, shift):
-    value = ref[channel]
-    if shift[0]:
-        value = pltpu.roll(value, shift[0] % value.shape[0], 0)
-    if shift[1]:
-        value = pltpu.roll(value, shift[1] % value.shape[1], 1)
-    return value
-
-
-def collide_tiles(load, solid_ref, store, first_row, rows, coefficients):
-    matrices, cross, push = coefficients
-
-    def body(t, carry):
-        row = pl.multiple_of(first_row + t * ROWS, ROWS)
-        for lane in range(0, solid_ref.shape[1], LANES):
-            where = (pl.ds(row, ROWS), pl.ds(lane, LANES))
-            ahead, back, flat = load(where)
-            solid = solid_ref[where] == 1
-            store(where, *relax(ahead, back, flat, solid, matrices, cross, push))
-        return carry
-
-    lax.fori_loop(0, rows // ROWS, body, 0)
-
-
-def first_kernel(f_ref, mask_ref, rates_ref, force_ref, off_ref, on_ref, flat_ref, f, solid, out, sems):
-    height = solid.shape[0]
-    rows = height // PIECES
-    copies = []
-    for piece in range(PIECES):
-        part = pl.ds(piece * rows, rows)
-        copies.append(
-            (
-                pltpu.make_async_copy(f_ref.at[:, part, :], f.at[:, part, :], sems.at[0, piece]),
-                pltpu.make_async_copy(mask_ref.at[part, :], solid.at[part, :], sems.at[1, piece]),
-            )
+def shift_in_z(halves, step):
+    if step == 0:
+        return halves
+    lane = lax.broadcasted_iota(jnp.int32, halves[0].shape, 1)
+    edge = lane == (0 if step > 0 else LANES - 1)
+    low, high = (pltpu.roll(value, step % LANES, 1) for value in halves)
+    return jnp.where(edge, high, low), jnp.where(edge, low, high)
+
+
+def relax_tile(load, solid_ref, solid_row, coefficients):
+    halves = []
+    for lane in range(0, solid_ref.shape[1], LANES):
+        solid = solid_ref[pl.ds(solid_row, ROWS), pl.ds(lane, LANES)] == 1
+        ahead, back, flat = relax(*load(lane), solid, *coefficients)
+        halves.append(ahead + back + flat)
+    return list(zip(*halves, strict=True))
+
+
+def first_kernel(
+    start, f_ref, mask_ref, rates_hbm, force_hbm, off_ref, on_ref, flat_ref, f, solid, out, rates, force, sems
+):
+    height = mask_ref.shape[0]
+    tiles = off_ref.shape[1] // ROWS + 2
+
+    def fetch(i):
+        row = (start + (i - 1) * ROWS) % height
+        return pltpu.make_async_copy(
+            f_ref.at[:, pl.ds(row, ROWS), :], f.at[:, pl.ds(i * ROWS, ROWS), :], sems.at[i]
         )
-        for copy in copies[-1]:
-            copy.start()
+
+    small = [
+        pltpu.make_async_copy(rates_hbm, rates, sems.at[tiles]),
+        pltpu.make_async_copy(force_hbm, force, sems.at[tiles + 1]),
+        pltpu.make_async_copy(mask_ref, solid, sems.at[tiles + 2]),
+    ]
+    fetch(0).start()
+    for copy in small:
+        copy.start()
+    for i in range(1, tiles):
+        fetch(i).start()
     side = local_frame()
-    coefficients = scalars(rates_ref, force_ref, side)
     toward = [select_channel(side, k) for k in range(5)]
     away = [select_channel(1 - side, k) for k in range(5)]
-
-    def load(where):
-        return (
-            [f[(toward[k], *where)] for k in range(5)],
-            [f[(away[k], *where)] for k in range(5)],
-            [f[(FLAT[k], *where)] for k in range(9)],
-        )
-
-    def store(where, ahead, back, flat):
-        for k, value in enumerate(ahead + back + flat):
-            out[(k, *where)] = value
-
-    for piece in range(PIECES):
-        for copy in copies[piece]:
-            copy.wait()
-        collide_tiles(load, solid, store, piece * rows, rows, coefficients)
-    finish(out, off_ref, on_ref, flat_ref)
-
-
-def finish(out, off_ref, on_ref, flat_ref):
-    for k in range(5):
-        off_ref[k] = shifted(out, k, GROUP_SHIFTS[k])
-    for k in range(5):
-        on_ref[k] = shifted(out, 5 + k, GROUP_SHIFTS[k])
-    for k in range(9):
-        flat_ref[k] = shifted(out, 10 + k, FLAT_SHIFTS[k])
+    channels = toward + away + list(FLAT)
+    for copy in small:
+        copy.wait()
+    coefficients = scalars(rates, force, side)
+    targets = [(off_ref, k) for k in range(5)] + [(on_ref, k) for k in range(5)]
+    targets += [(flat_ref, k) for k in range(9)]
+    shifts = GROUP_SHIFTS + GROUP_SHIFTS + FLAT_SHIFTS
+
+    def collide(i):
+        local = pl.multiple_of(i * ROWS, ROWS)
+        pltpu.make_async_copy(
+            f_ref.at[:, pl.ds(0, ROWS), :], f.at[:, pl.ds(local, ROWS), :], sems.at[i]
+        ).wait()
+
+        def load(lane):
+            values = [f[c, pl.ds(local, ROWS), pl.ds(lane, LANES)] for c in channels]
+            return values[:5], values[5:10], values[10:]
+
+        row = pl.multiple_of(lax.rem(start + height + (i - 1) * ROWS, height), ROWS)
+        for k, pair in enumerate(relax_tile(load, solid, row, coefficients)):
+            for half in range(2):
+                out[k, half, pl.ds(local, ROWS), :] = pair[half]
+
+    def emit(i):
+        local = i * ROWS
+        row = pl.multiple_of(local - ROWS, ROWS)
+        for k, (ref, entry) in enumerate(targets):
+            pair = tuple(out[k, half, pl.ds(local - shifts[k][0], ROWS), :] for half in range(2))
+            pair = shift_in_z(pair, shifts[k][1])
+            for half in range(2):
+                ref[entry, pl.ds(row, ROWS), pl.ds(half * LANES, LANES)] = pair[half]
+
+    def head(i, carry):
+        collide(i)
+        return carry
+
+    def body(i, carry):
+        emit(i - 2)
+        collide(i)
+        return carry
+
+    lax.fori_loop(0, 3, head, 0)
+    lax.fori_loop(3, tiles, body, 0)
+    emit(tiles - 2)
 
 
 def second_kernel(
-    off_in, on_in, flat_in, mask_ref, rates_ref, force_ref, off_ref, on_ref, out_ref, solid, out, moved, sems
+    start, off_in, on_in, flat_in, solid, rates, force, off_ref, on_ref, flat_ref
 ):
-    copy = pltpu.make_async_copy(mask_ref, solid, sems.at[0])
-    copy.start()
-    side = local_frame()
-    coefficients = scalars(rates_ref, force_ref, side)
-
-    def load(where):
-        return (
-            [on_in[(k, *where)] for k in range(5)],
-            [off_in[(k, *where)] for k in range(5)],
-            [flat_in[(k, *where)] for k in range(9)],
-        )
-
-    def store(where, ahead, back, flat):
-        for k, value in enumerate(ahead + back + flat):
-            out[(k, *where)] = value
-
-    copy.wait()
-    collide_tiles(load, solid, store, 0, solid.shape[0], coefficients)
-    finish(out, off_ref, on_ref, moved)
-    copies = [
-        pltpu.make_async_copy(moved.at[k], out_ref.at[FLAT[k]], sems.at[1 + k]) for k in range(9)
-    ]
-    for copy in copies:
-        copy.start()
+    coefficients = scalars(rates, force, local_frame())
+    targets = [(off_ref, k) for k in range(5)] + [(on_ref, k) for k in range(5)]
+    targets += [(flat_ref, k) for k in range(9)]
+    shifts = GROUP_SHIFTS + GROUP_SHIFTS + FLAT_SHIFTS
+
+    def body(i, carry):
+        local = pl.multiple_of(i * ROWS, ROWS)
+
+        def load(lane):
+            where = (pl.ds(local, ROWS), pl.ds(lane, LANES))
+            return (
+                [on_in[(k, *where)] for k in range(5)],
+                [off_in[(k, *where)] for k in range(5)],
+                [flat_in[(k, *where)] for k in range(9)],
+            )
+
+        row = pl.multiple_of(start + local, ROWS)
+        for k, pair in enumerate(relax_tile(load, solid, row, coefficients)):
+            ref, entry = targets[k]
+            pair = shift_in_z(pair, shifts[k][1])
+            for half in range(2):
+                ref[entry, pl.ds(local, ROWS), pl.ds(half * LANES, LANES)] = pair[half]
+        return carry
+
+    lax.fori_loop(0, off_in.shape[1] // ROWS, body, 0)
+
+
+def place(low_ref, high_ref, out_ref, moved, sems, number_of, shifts):
+    copies = []
+    part = low_ref.shape[1]
+    slot = 0
+    for k, (step, _) in enumerate(shifts):
+        if step == 0:
+            for half, ref in enumerate((low_ref, high_ref)):
+                rows = pl.ds(half * part, part)
+                copies.append(
+                    pltpu.make_async_copy(
+                        ref.at[k], out_ref.at[number_of(k), rows, :], sems.at[2 * k + half]
+                    )
+                )
+                copies[-1].start()
+    for k, (step, _) in enumerate(shifts):
+        if step != 0:
+            both = jnp.concatenate([low_ref[k], high_ref[k]], axis=0)
+            moved[slot] = pltpu.roll(both, step % both.shape[0], 0)
+            copies.append(
+                pltpu.make_async_copy(moved.at[slot], out_ref.at[number_of(k)], sems.at[2 * k])
+            )
+            copies[-1].start()
+            slot += 1
     for copy in copies:
         copy.wait()
 
 
-def place_kernel(own, group_ref, out_in, out_ref, sems):
+def place_flat_kernel(low_ref, high_ref, out_ref, moved, sems):
+    place(low_ref, high_ref, out_ref, moved, sems, lambda k: FLAT[k], FLAT_SHIFTS)
+
+
+def place_group_kernel(own, low_ref, high_ref, out_in, out_ref, moved, sems):
     del out_in
     side = local_frame()
     side = 1 - side if own else side
-    copies = [
-        pltpu.make_async_copy(group_ref.at[k], out_ref.at[select_channel(side, k)], sems.at[k])
-        for k in range(5)
-    ]
-    for copy in copies:
-        copy.start()
-    for copy in copies:
-        copy.wait()
+    place(low_ref, high_ref, out_ref, moved, sems, lambda k: select_channel(side, k), GROUP_SHIFTS)
 
 
 def in_vmem(array):
@@ -365,73 +407,100 @@
     return pltpu.CompilerParams(vmem_limit_bytes=mebibytes << 20)
 
 
+def in_smem(array):
+    return pltpu.with_memory_space_constraint(array, pltpu.SMEM)
+
+
 def on_device(populations, solid_mask, relax_rates, body_force):
     channels, depth, height, breadth = populations.shape
-    assert depth == 1
+    assert depth == 1 and breadth == 2 * LANES
     count = lax.axis_size("gx")
     assert count % 2 == 0
     off_pairs = [(i, (i + 1) % count if i % 2 else (i - 1) % count) for i in range(count)]
     on_pairs = [(i, i ^ 1) for i in range(count)]
     plane = in_hbm(populations.reshape(channels, height, breadth))
-    mask = in_hbm(solid_mask.reshape(height, breadth))
-    relax_rates, body_force = in_hbm(relax_rates), in_hbm(body_force)
+    mask = solid_mask.reshape(height, breadth)
     f32 = jnp.float32
-    group = vmem_result((5, height, breadth))
-    whole = hbm_result((channels, height, breadth))
+    part = height // PARTS
     anywhere = pl.BlockSpec(memory_space=pl.ANY)
     local = pl.BlockSpec(memory_space=pltpu.VMEM)
     small = pl.BlockSpec(memory_space=pltpu.SMEM)
-    sheet = pltpu.VMEM((height, breadth), jnp.int32)
-    nodes = height * breadth
-    off, on, flat = pl.pallas_call(
-        first_kernel,
-        out_shape=(group, group, vmem_result((9, height, breadth))),
-        in_specs=[anywhere, anywhere, small, small],
-        out_specs=(local, local, local),
-        scratch_shapes=[
-            pltpu.VMEM((channels, height, breadth), f32),
-            sheet,
-            pltpu.VMEM((channels, height, breadth), f32),
-            pltpu.SemaphoreType.DMA((2, PIECES)),
-        ],
+    pieces = tuple(vmem_result((n, part, breadth)) for n in (5, 5, 9))
+    whole = hbm_result((channels, height, breadth))
+    tiles = part // ROWS + 2
+
+    def cost(rows):
+        nodes = rows * breadth
+        return pl.CostEstimate(flops=320 * nodes, bytes_accessed=160 * nodes, transcendentals=0)
+
+    def step_one(p):
+        return pl.pallas_call(
+            functools.partial(first_kernel, p * part),
+            out_shape=pieces,
+            in_specs=[anywhere] * 4,
+            out_specs=(local, local, local),
+            scratch_shapes=[
+                pltpu.VMEM((channels, tiles * ROWS, breadth), f32),
+                pltpu.VMEM((height, breadth), jnp.int32),
+                pltpu.VMEM((channels, 2, tiles * ROWS, LANES), f32),
+                pltpu.SMEM(relax_rates.shape, f32),
+                pltpu.SMEM(body_force.shape, f32),
+                pltpu.SemaphoreType.DMA((tiles + 3,)),
+            ],
+            cost_estimate=cost(part),
+            compiler_params=params(8),
+        )(plane, in_hbm(mask), in_hbm(relax_rates), in_hbm(body_force))
+
+    def step_two(p, off, on, flat):
+        return pl.pallas_call(
+            functools.partial(second_kernel, p * part),
+            out_shape=pieces,
+            in_specs=[local, local, local, local, small, small],
+            out_specs=(local, local, local),
+            cost_estimate=cost(part),
+            compiler_params=params(8),
+        )(in_vmem(off), in_vmem(on), flat, in_vmem(mask), in_smem(relax_rates), in_smem(body_force))
+
+    def send(array, pairs):
+        return lax.ppermute(array, "gx", pairs)
+
+    offs, ons, flats = [], [], []
+    for p in range(PARTS):
+        off, on, flat = step_one(p)
+        offs.append(send(off, off_pairs))
+        ons.append(send(on, on_pairs))
+        flats.append(flat)
+    last = []
+    for p in range(PARTS):
+        off, on, flat = step_two(p, offs[p], ons[p], flats[p])
+        last.append((send(off, off_pairs), on, flat))
+    offs, ons, flats = zip(*last, strict=True)
+    ons = [send(on, on_pairs) for on in ons]
+    result = pl.pallas_call(
+        place_flat_kernel,
+        out_shape=whole,
+        in_specs=[local, local],
+        out_specs=anywhere,
+        scratch_shapes=[pltpu.VMEM((6, height, breadth), f32), pltpu.SemaphoreType.DMA((18,))],
         cost_estimate=pl.CostEstimate(
-            flops=320 * nodes, bytes_accessed=80 * nodes, transcendentals=0
+            flops=0, bytes_accessed=36 * height * breadth, transcendentals=0
         ),
-        compiler_params=params(14),
-        name="first_step",
-    )(plane, mask, relax_rates, body_force)
-    off = lax.ppermute(off, "gx", off_pairs)
-    on = lax.ppermute(on, "gx", on_pairs)
-    off, on, result = pl.pallas_call(
-        second_kernel,
-        out_shape=(group, group, whole),
-        in_specs=[local, local, local, anywhere, small, small],
-        out_specs=(local, local, anywhere),
-        scratch_shapes=[
-            sheet,
-            pltpu.VMEM((channels, height, breadth), f32),
-            pltpu.VMEM((9, height, breadth), f32),
-            pltpu.SemaphoreType.DMA((10,)),
-        ],
-        cost_estimate=pl.CostEstimate(
-            flops=320 * nodes, bytes_accessed=80 * nodes, transcendentals=0
-        ),
-        compiler_params=params(14),
-        name="second_step",
-    )(in_vmem(off), in_vmem(on), flat, mask, relax_rates, body_force)
-    off = lax.ppermute(off, "gx", off_pairs)
-    on = lax.ppermute(on, "gx", on_pairs)
-    for own, arrived in ((False, on), (True, off)):
+        compiler_params=params(4),
+        name="place_flat",
+    )(*flats)
+    for own, arrived in ((False, ons), (True, offs)):
         result = pl.pallas_call(
-            functools.partial(place_kernel, own),
+            functools.partial(place_group_kernel, own),
             out_shape=whole,
-            in_specs=[local, anywhere],
+            in_specs=[local, local, anywhere],
             out_specs=anywhere,
-            scratch_shapes=[pltpu.SemaphoreType.DMA((5,))],
-            input_output_aliases={1: 0},
-            cost_estimate=pl.CostEstimate(flops=0, bytes_accessed=20 * nodes, transcendentals=0),
+            scratch_shapes=[pltpu.VMEM((2, height, breadth), f32), pltpu.SemaphoreType.DMA((10,))],
+            input_output_aliases={2: 0},
+            cost_estimate=pl.CostEstimate(
+                flops=0, bytes_accessed=20 * height * breadth, transcendentals=0
+            ),
             compiler_params=params(4),
-        )(in_vmem(arrived), result)
+        )(*(in_vmem(array) for array in arrived), result)
     return result.reshape(channels, depth, height, breadth)
 
 

time: 44.8 us -> 41.6 us (0.929)
  waiting for transfers between devices: 26.8 us -> 20.3 us
  Pallas kernels: 10.4 us -> 12.7 us
  starting transfers between devices: 7.4 us -> 8.29 us
    ppermute x4 -> x8, waiting for transfers between devices: 26.8 us -> 20.3 us  [send(): return lax.ppermute(array, 'gx', pairs)]
    pallas_call x4 -> x7, Pallas kernels: 10.4 us -> 12.7 us  [the longest x2 5.7 us: step_one(): pl.pallas_call(functools.partial(first_kernel, p * part), out_shape=piece...]
    ppermute x4 -> x8, starting transfers between devices: 7.4 us -> 8.29 us  [send(): return lax.ppermute(array, 'gx', pairs)]
  transfers between devices with their start and end apart: 4 -> 8, of which waited for: 3 -> 4; matrix products, arithmetic and copies ran while one was open for 0% -> 0% of each run, Pallas kernels for 2% -> 22%
where the time goes in v1:
time: 41.6 us; the launch traced here: 41.4 us
  waiting for transfers between devices  20.3 us (49%)
  Pallas kernels  12.7 us (31%)
  starting transfers between devices  8.29 us (20%)
    ppermute x8, waiting for transfers between devices, send(): return lax.ppermute(array, 'gx', pairs)  20.3 us
    ppermute x8, starting transfers between devices, send(): return lax.ppermute(array, 'gx', pairs)  8.29 us
    pallas_call x2, Pallas kernels, step_one(): pl.pallas_call(functools.partial(first_kernel, p * part), out_shape=piece...  5.7 us
    pallas_call x2, Pallas kernels, step_two(): pl.pallas_call(functools.partial(second_kernel, p * part), out_shape=piec...  3.99 us
    pallas_call x2, Pallas kernels, on_device(): pl.pallas_call(functools.partial(place_group_kernel, own), out_shape=whol...  1.86 us
    pallas_call x1, Pallas kernels, on_device(): pl.pallas_call(place_flat_kernel, out_shape=whole, in_specs=[local, local...  1.16 us
  transfers between devices with their start and end apart: 8, of which 4 were waited for; matrix products, arithmetic and copies ran while one was open for 0% of the time, Pallas kernels for 22%

profile of v1, /device:TPU:1, one launch (start us, length us, event | category | flops | bytes accessed | tf_op | source)
XLA Modules:
  0.0 41.4 jit_solution(10504672895120245182)
XLA Ops:
  0.0 2.9 %shard_map.48 = (f32[5,64,256]{2,1,0:T(8,128)S(1)}, f32[5,64,256]{2,1,0:T(8,128)S(1)}, f32[9,64,256]{2,1,0:T(8,128)S(1)}) custom-call(f32[19,128,256]{2,1,0:T(8,128)} %bitcast.9, s32[128,256]{1,0:T(8,128)} %bitcast.5, f32[19]{0:T(128)} %rates.3, f32[3]{0:T(128)} %force.3), custom_call_target="tpu_custom_call" | custom-call | flops 5242880 | bytes 2621440 | tf_op jit(solution)/shard_map/pallas_call | solution.py:437
  2.9 2.7 %collective-permute-start.3 = (f32[5,64,256]{2,1,0:T(8,128)S(1)}, f32[5,64,256]{2,1,0:T(8,128)S(1)}, u32[]{:S(2)}, u32[]{:S(2)}) collective-permute-start(f32[5,64,256]{2,1,0:T(8,128)S(1)} %get-tuple-element.21), channel_id=1, source_target_pairs={{0,15},{1,2},{2,1},{3,4},{4,3},{5,6},{6,5},{7,8},{8,7},{9,10},{10,... | collective-permute-start | bytes 983048 | tf_op jit(solution)/shard_map/ppermute | solution.py:465
  5.5 2.9 %collective-permute-start.4 = (f32[5,64,256]{2,1,0:T(8,128)S(1)}, f32[5,64,256]{2,1,0:T(8,128)S(1)}, u32[]{:S(2)}, u32[]{:S(2)}) collective-permute-start(f32[5,64,256]{2,1,0:T(8,128)S(1)} %get-tuple-element.22), channel_id=1, source_target_pairs={{0,1},{1,0},{2,3},{3,2},{4,5},{5,4},{6,7},{7,6},{8,9},{9,8},{10,11... | collective-permute-start | bytes 983048 | tf_op jit(solution)/shard_map/ppermute | solution.py:465
  8.4 2.8 %shard_map.46 = (f32[5,64,256]{2,1,0:T(8,128)S(1)}, f32[5,64,256]{2,1,0:T(8,128)S(1)}, f32[9,64,256]{2,1,0:T(8,128)S(1)}) custom-call(f32[19,128,256]{2,1,0:T(8,128)} %bitcast.10, s32[128,256]{1,0:T(8,128)} %bitcast.6, f32[19]{0:T(128)} %rates.3, f32[3]{0:T(128)} %force.3), custom_call_target="tpu_custom_call" | custom-call | flops 5242880 | bytes 2621440 | tf_op jit(solution)/shard_map/pallas_call | solution.py:437
  11.3 0.1 collective-permute-start
  11.3 0.7 %collective-permute-start.1 = (f32[5,64,256]{2,1,0:T(8,128)S(1)}, f32[5,64,256]{2,1,0:T(8,128)S(1)}, u32[]{:S(2)}, u32[]{:S(2)}) collective-permute-start(f32[5,64,256]{2,1,0:T(8,128)S(1)} %get-tuple-element.18), channel_id=1, source_target_pairs={{0,1},{1,0},{2,3},{3,2},{4,5},{5,4},{6,7},{7,6},{8,9},{9,8},{10,11... | collective-permute-start | bytes 983048 | tf_op jit(solution)/shard_map/ppermute | solution.py:465
  12.1 4.5 %collective-permute-done.3.off_in = f32[5,64,256]{2,1,0:T(8,128)S(1)} collective-permute-done((f32[5,64,256]{2,1,0:T(8,128)S(1)}, f32[5,64,256]{2,1,0:T(8,128)S(1)}, u32[]{:S(2)}, u32[]{:S(2)}) %collective-permute-start.3) | collective-permute-done | bytes 327712 | tf_op jit(solution)/shard_map/ppermute | solution.py:465
  16.6 0.0 collective-permute-done.4.on_in
  16.6 0.0 copy-done
  16.6 2.0 %shard_map.49 = (f32[5,64,256]{2,1,0:T(8,128)S(1)}, f32[5,64,256]{2,1,0:T(8,128)S(1)}, f32[9,64,256]{2,1,0:T(8,128)S(1)}) custom-call(f32[5,64,256]{2,1,0:T(8,128)S(1)} %collective-permute-done.3.off_in, f32[5,64,256]{2,1,0:T(8,128)S(1)} %collective-permute-done.4.on_in, f32[9,64,256]{2,1,0:T(8,128)S(1)} %get-tuple-element.23.flat_in, ...), custom_call_target="tpu_custom_call" | custom-call | flops 5242880 | bytes 2621440 | tf_op jit(solution)/shard_map/pallas_call | solution.py:455
  18.6 0.1 collective-permute-start.7
  18.7 2.6 %collective-permute-done.off_in = f32[5,64,256]{2,1,0:T(8,128)S(1)} collective-permute-done((f32[5,64,256]{2,1,0:T(8,128)S(1)}, f32[5,64,256]{2,1,0:T(8,128)S(1)}, u32[]{:S(2)}, u32[]{:S(2)}) %collective-permute-start) | collective-permute-done | bytes 327712 | tf_op jit(solution)/shard_map/ppermute | solution.py:465
  21.3 0.0 collective-permute-done.1.on_in
  21.3 2.0 %shard_map.47 = (f32[5,64,256]{2,1,0:T(8,128)S(1)}, f32[5,64,256]{2,1,0:T(8,128)S(1)}, f32[9,64,256]{2,1,0:T(8,128)S(1)}) custom-call(f32[5,64,256]{2,1,0:T(8,128)S(1)} %collective-permute-done.off_in, f32[5,64,256]{2,1,0:T(8,128)S(1)} %collective-permute-done.1.on_in, f32[9,64,256]{2,1,0:T(8,128)S(1)} %get-tuple-element.19.flat_in, s32[128,256]{1,0:T(8,128)S(1)} %bitcast.8, ...), custom_call_target="tpu_custom_call" | custom-call | flops 5242880 | bytes 2621440 | tf_op jit(solution)/shard_map/pallas_call | solution.py:455
  23.3 0.1 collective-permute-start.6
  23.4 1.3 %collective-permute-start.5 = (f32[5,64,256]{2,1,0:T(8,128)S(1)}, f32[5,64,256]{2,1,0:T(8,128)S(1)}, u32[]{:S(2)}, u32[]{:S(2)}) collective-permute-start(f32[5,64,256]{2,1,0:T(8,128)S(1)} %get-tuple-element.24), channel_id=1, source_target_pairs={{0,15},{1,2},{2,1},{3,4},{4,3},{5,6},{6,5},{7,8},{8,7},{9,10},{10,... | collective-permute-start | bytes 983048 | tf_op jit(solution)/shard_map/ppermute | solution.py:465
  24.7 0.5 %collective-permute-start.2 = (f32[5,64,256]{2,1,0:T(8,128)S(1)}, f32[5,64,256]{2,1,0:T(8,128)S(1)}, u32[]{:S(2)}, u32[]{:S(2)}) collective-permute-start(f32[5,64,256]{2,1,0:T(8,128)S(1)} %get-tuple-element.20), channel_id=1, source_target_pairs={{0,15},{1,2},{2,1},{3,4},{4,3},{5,6},{6,5},{7,8},{8,7},{9,10},{10,... | collective-permute-start | bytes 983048 | tf_op jit(solution)/shard_map/ppermute | solution.py:465
  25.2 1.2 %place_flat.1.out_in = f32[19,128,256]{2,1,0:T(8,128)} custom-call(f32[9,64,256]{2,1,0:T(8,128)S(1)} %get-tuple-element.27.low_ref, f32[9,64,256]{2,1,0:T(8,128)S(1)} %get-tuple-element.28.high_ref), custom_call_target="tpu_custom_call" | custom-call | bytes 1179648 | tf_op jit(solution)/shard_map/place_flat/pallas_call | solution.py:479
  26.4 0.0 collective-permute-done.7.high_ref
  26.4 0.0 collective-permute-done.6.low_ref
  26.4 0.9 %shard_map.50.out_in = f32[19,128,256]{2,1,0:T(8,128)} custom-call(f32[5,64,256]{2,1,0:T(8,128)S(1)} %collective-permute-done.6.low_ref, f32[5,64,256]{2,1,0:T(8,128)S(1)} %collective-permute-done.7.high_ref, f32[19,128,256]{2,1,0:T(8,128)} %place_flat.1.out_in), custom_call_target="tpu_custom_call", output_to_operand_aliasing={{}: (2, {})} | custom-call | bytes 655360 | tf_op jit(solution)/shard_map/pallas_call | solution.py:492
  27.3 9.7 %collective-permute-done.5.high_ref = f32[5,64,256]{2,1,0:T(8,128)S(1)} collective-permute-done((f32[5,64,256]{2,1,0:T(8,128)S(1)}, f32[5,64,256]{2,1,0:T(8,128)S(1)}, u32[]{:S(2)}, u32[]{:S(2)}) %collective-permute-start.5) | collective-permute-done | bytes 327712 | tf_op jit(solution)/shard_map/ppermute | solution.py:465
  37.0 3.5 %collective-permute-done.2.low_ref = f32[5,64,256]{2,1,0:T(8,128)S(1)} collective-permute-done((f32[5,64,256]{2,1,0:T(8,128)S(1)}, f32[5,64,256]{2,1,0:T(8,128)S(1)}, u32[]{:S(2)}, u32[]{:S(2)}) %collective-permute-start.2) | collective-permute-done | bytes 327712 | tf_op jit(solution)/shard_map/ppermute | solution.py:465
  40.5 0.9 %shard_map.51 = f32[19,128,256]{2,1,0:T(8,128)} custom-call(f32[5,64,256]{2,1,0:T(8,128)S(1)} %collective-permute-done.2.low_ref, f32[5,64,256]{2,1,0:T(8,128)S(1)} %collective-permute-done.5.high_ref, f32[19,128,256]{2,1,0:T(8,128)} %shard_map.50.out_in), custom_call_target="tpu_custom_call", output_to_operand_aliasing={{}: (2, {})} | custom-call | bytes 655360 | tf_op jit(solution)/shard_map/pallas_call | solution.py:492
  (5 shorter events, 0.0 us)
Async XLA Ops:
  0.0 16.6 %copy-start = (s32[1,128,256]{2,1,0:T(8,128)S(1)}, s32[1,128,256]{2,1,0:T(8,128)}, u32[]{:S(2)}) copy-start(s32[1,128,256]{2,1,0:T(8,128)} %param.5) | copy-start | bytes 393220
  0.0 16.6 %copy-start.1 = (f32[19]{0:T(128)S(1)}, f32[19]{0:T(128)}, u32[]{:S(2)}) copy-start(f32[19]{0:T(128)} %rates.3) | copy-start | bytes 232
  0.0 16.6 %copy-start.2 = (f32[3]{0:T(128)S(1)}, f32[3]{0:T(128)}, u32[]{:S(2)}) copy-start(f32[3]{0:T(128)} %force.3) | copy-start | bytes 40
  2.9 13.7 %collective-permute-start.3 = (f32[5,64,256]{2,1,0:T(8,128)S(1)}, f32[5,64,256]{2,1,0:T(8,128)S(1)}, u32[]{:S(2)}, u32[]{:S(2)}) collective-permute-start(f32[5,64,256]{2,1,0:T(8,128)S(1)} %get-tuple-element.21), channel_id=1, source_target_pairs={{0,15},{1,2},{2,1},{3,4},{4,3},{5,6},{6,5},{7,8},{8,7},{9,10},{10,... | collective-permute-start | bytes 983048 | tf_op jit(solution)/shard_map/ppermute | solution.py:465
  5.5 11.0 %collective-permute-start.4 = (f32[5,64,256]{2,1,0:T(8,128)S(1)}, f32[5,64,256]{2,1,0:T(8,128)S(1)}, u32[]{:S(2)}, u32[]{:S(2)}) collective-permute-start(f32[5,64,256]{2,1,0:T(8,128)S(1)} %get-tuple-element.22), channel_id=1, source_target_pairs={{0,1},{1,0},{2,3},{3,2},{4,5},{5,4},{6,7},{7,6},{8,9},{9,8},{10,11... | collective-permute-start | bytes 983048 | tf_op jit(solution)/shard_map/ppermute | solution.py:465
  11.3 10.1 %collective-permute-start = (f32[5,64,256]{2,1,0:T(8,128)S(1)}, f32[5,64,256]{2,1,0:T(8,128)S(1)}, u32[]{:S(2)}, u32[]{:S(2)}) collective-permute-start(f32[5,64,256]{2,1,0:T(8,128)S(1)} %get-tuple-element.17), channel_id=1, source_target_pairs={{0,15},{1,2},{2,1},{3,4},{4,3},{5,6},{6,5},{7,8},{8,7},{9,10},{10,... | collective-permute-start | bytes 983048 | tf_op jit(solution)/shard_map/ppermute | solution.py:465
  11.3 10.0 %collective-permute-start.1 = (f32[5,64,256]{2,1,0:T(8,128)S(1)}, f32[5,64,256]{2,1,0:T(8,128)S(1)}, u32[]{:S(2)}, u32[]{:S(2)}) collective-permute-start(f32[5,64,256]{2,1,0:T(8,128)S(1)} %get-tuple-element.18), channel_id=1, source_target_pairs={{0,1},{1,0},{2,3},{3,2},{4,5},{5,4},{6,7},{7,6},{8,9},{9,8},{10,11... | collective-permute-start | bytes 983048 | tf_op jit(solution)/shard_map/ppermute | solution.py:465
  18.6 7.8 %collective-permute-start.7 = (f32[5,64,256]{2,1,0:T(8,128)S(1)}, f32[5,64,256]{2,1,0:T(8,128)S(1)}, u32[]{:S(2)}, u32[]{:S(2)}) collective-permute-start(f32[5,64,256]{2,1,0:T(8,128)S(1)} %get-tuple-element.26), channel_id=1, source_target_pairs={{0,1},{1,0},{2,3},{3,2},{4,5},{5,4},{6,7},{7,6},{8,9},{9,8},{10,11... | collective-permute-start | bytes 983048 | tf_op jit(solution)/shard_map/ppermute | solution.py:465
  23.3 3.1 %collective-permute-start.6 = (f32[5,64,256]{2,1,0:T(8,128)S(1)}, f32[5,64,256]{2,1,0:T(8,128)S(1)}, u32[]{:S(2)}, u32[]{:S(2)}) collective-permute-start(f32[5,64,256]{2,1,0:T(8,128)S(1)} %get-tuple-element.25), channel_id=1, source_target_pairs={{0,1},{1,0},{2,3},{3,2},{4,5},{5,4},{6,7},{7,6},{8,9},{9,8},{10,11... | collective-permute-start | bytes 983048 | tf_op jit(solution)/shard_map/ppermute | solution.py:465
  23.4 13.6 %collective-permute-start.5 = (f32[5,64,256]{2,1,0:T(8,128)S(1)}, f32[5,64,256]{2,1,0:T(8,128)S(1)}, u32[]{:S(2)}, u32[]{:S(2)}) collective-permute-start(f32[5,64,256]{2,1,0:T(8,128)S(1)} %get-tuple-element.24), channel_id=1, source_target_pairs={{0,15},{1,2},{2,1},{3,4},{4,3},{5,6},{6,5},{7,8},{8,7},{9,10},{10,... | collective-permute-start | bytes 983048 | tf_op jit(solution)/shard_map/ppermute | solution.py:465
  24.7 15.8 %collective-permute-start.2 = (f32[5,64,256]{2,1,0:T(8,128)S(1)}, f32[5,64,256]{2,1,0:T(8,128)S(1)}, u32[]{:S(2)}, u32[]{:S(2)}) collective-permute-start(f32[5,64,256]{2,1,0:T(8,128)S(1)} %get-tuple-element.20), channel_id=1, source_target_pairs={{0,15},{1,2},{2,1},{3,4},{4,3},{5,6},{6,5},{7,8},{8,7},{9,10},{10,... | collective-permute-start | bytes 983048 | tf_op jit(solution)/shard_map/ppermute | solution.py:465

commit v2 on v1

v2 whole, which is shorter than its diff:
```python
import functools

import jax
import jax.numpy as jnp
import numpy as np
from jax import lax
from jax.experimental import pallas as pl
from jax.experimental.pallas import tpu as pltpu
from jax.sharding import PartitionSpec as P

EIGHTHS = (4, 4)
COEFFICIENTS = 52
GROUPS = (0, 2, 5)
LANES = 128
ROWS = 8

UP = (1, 7, 9, 11, 13)
DOWN = (2, 10, 8, 14, 12)
GROUP_SHIFTS = ((0, 0), (1, 0), (-1, 0), (0, 1), (0, -1))
BOUNCE = (0, 2, 1, 4, 3)
FLAT = (0, 3, 4, 5, 6, 15, 16, 17, 18)
FLAT_SHIFTS = ((0, 0), (1, 0), (-1, 0), (0, 1), (0, -1), (1, 1), (-1, -1), (1, -1), (-1, 1))
FLAT_OPPOSITE = (0, 2, 1, 4, 3, 6, 5, 8, 7)


def moment_tables():
    velocities = np.array(
        [
            [0, 0, 0],
            [1, 0, 0],
            [-1, 0, 0],
            [0, 1, 0],
            [0, -1, 0],
            [0, 0, 1],
            [0, 0, -1],
            [1, 1, 0],
            [-1, -1, 0],
            [1, -1, 0],
            [-1, 1, 0],
            [1, 0, 1],
            [-1, 0, -1],
            [1, 0, -1],
            [-1, 0, 1],
            [0, 1, 1],
            [0, -1, -1],
            [0, 1, -1],
            [0, -1, 1],
        ]
    )
    x, y, z = velocities.T
    polynomials = np.stack(
        [
            np.ones(19),
            x,
            y,
            z,
            x * y,
            x * z,
            y * z,
            x**2,
            y**2,
            z**2,
            x * y**2,
            x * z**2,
            x**2 * y,
            x**2 * z,
            y * z**2,
            y**2 * z,
            x**2 * y**2,
            x**2 * z**2,
            y**2 * z**2,
        ]
    ).astype(np.float64)
    basis = []
    for row in polynomials:
        vector = row.copy()
        for earlier in basis:
            vector = vector - vector @ earlier / (earlier @ earlier) * earlier
        basis.append(vector)
    moments = np.stack(basis)
    classes = ((0, 7, 8, 9, 16, 17, 18), (1, 10, 11), (2, 12, 14), (3, 13, 15))
    tables = []
    for numbers in classes:
        rows = list(numbers)
        lower = moments[rows] @ np.linalg.pinv(polynomials[rows])
        lower = np.where(np.abs(lower) < 1e-12, 0.0, lower)
        inverse = np.linalg.inv(lower)
        inverse = np.where(np.abs(inverse) < 1e-12, 0.0, inverse)
        tables.append((numbers, lower, inverse))
    return tables


def relaxing_entries(rates):
    matrices = []
    for numbers, lower, inverse in moment_tables():
        size = len(numbers)
        matrix = {}
        for i in range(size):
            for j in range(i + 1):
                total = None
                for m in range(j, i + 1):
                    factor = float(inverse[i, m] * lower[m, j])
                    if factor == 0.0:
                        continue
                    term = rates[numbers[m]] * factor
                    total = term if total is None else total + term
                if total is not None:
                    matrix[i, j] = total * 0.5 if i or size == 3 else total
        matrices.append(matrix)
    return matrices


def apply_lower(matrix, vector):
    out = []
    for i in range(len(vector)):
        total = None
        for j in range(i + 1):
            if (i, j) in matrix:
                term = matrix[i, j]() * vector[j]
                total = term if total is None else total + term
        out.append(total)
    return out


def relax(ahead, back, flat, solid, matrices, cross_rates, push):
    def butterfly(pp, pm, mp, mm):
        a, b, c, d = pp + pm, pp - pm, mp + mm, mp - mm
        return a + c, a - c, b + d, b - d

    sx, sy, sz = ahead[0] + back[0], flat[1] + flat[2], flat[3] + flat[4]
    xy, xy_x, xy_y, xy_xy = butterfly(ahead[1], ahead[2], back[1], back[2])
    xz, xz_x, xz_z, xz_xz = butterfly(ahead[3], ahead[4], back[3], back[4])
    yz, yz_y, yz_z, yz_yz = butterfly(flat[5], flat[7], flat[8], flat[6])
    density = (flat[0] + (sx + sy)) + ((sz + xy) + (xz + yz))
    jx = (ahead[0] - back[0]) + (xy_x + xz_x)
    jy = (flat[1] - flat[2]) + (xy_y + yz_y)
    jz = (flat[3] - flat[4]) + (xz_z + yz_z)
    over = 1.0 / density
    ux, uy, uz = jx * over, jy * over, jz * over
    qxx, qyy, qzz = jx * ux, jy * uy, jz * uz
    energy = 1.5 * (qxx + (qyy + qzz))
    still = density - energy
    base = still * (1.0 / 9.0)
    hx, hy, hz = 0.5 * qxx, 0.5 * qyy, 0.5 * qzz
    bx, by, bz = base + hx, base + hy, base + hz
    xy, xz, yz = xy - (bx + hy), xz - (bx + hz), yz - (by + hz)
    raw = [
        density - (still + energy),
        (sx - bx) + (xy + xz),
        (sy - by) + (xy + yz),
        (sz - bz) + (xz + yz),
        xy,
        xz,
        yz,
    ]
    total, mx, my, mz, cxy, cxz, cyz = apply_lower(matrices[0], raw)
    even_x, even_y, even_z = mx - (cxy + cxz), my - (cxy + cyz), mz - (cxz + cyz)
    rest = (mx + my) + ((mz - cxy) - (cxz + cyz))
    even_rest = total - (rest + rest)
    even_xy, even_xz, even_yz = 0.5 * cxy, 0.5 * cxz, 0.5 * cyz

    def odd_class(matrix, current, first, second, force):
        mean = current * (1.0 / 3.0)
        departures = [current - 3.0 * mean, first - mean, second - mean]
        along, first, second = apply_lower(matrix, departures)
        lift = density * force()
        along = along - (lift + (first + second))
        return along, 0.5 * (first - lift), 0.5 * (second - lift)

    odd_x, odd_xy_x, odd_xz_x = odd_class(matrices[1], jx, xy_x, xz_x, push[0])
    odd_y, odd_xy_y, odd_yz_y = odd_class(matrices[2], jy, xy_y, yz_y, push[1])
    odd_z, odd_xz_z, odd_yz_z = odd_class(matrices[3], jz, xz_z, yz_z, push[2])
    both_xy = (xy_xy - jx * uy) * cross_rates[0]()
    both_xz = (xz_xz - jx * uz) * cross_rates[1]()
    both_yz = (yz_yz - jy * uz) * cross_rates[2]()

    def spread(even, first, second, both):
        a, b, c, d = even + first, second + both, even - first, second - both
        return a + b, a - b, c + d, c - d

    xy_pp, xy_pm, xy_mp, xy_mm = spread(even_xy, odd_xy_x, odd_xy_y, both_xy)
    xz_pp, xz_pm, xz_mp, xz_mm = spread(even_xz, odd_xz_x, odd_xz_z, both_xz)
    yz_pp, yz_pm, yz_mp, yz_mm = spread(even_yz, odd_yz_y, odd_yz_z, both_yz)
    new_ahead = [even_x + odd_x, xy_pp, xy_pm, xz_pp, xz_pm]
    new_back = [even_x - odd_x, xy_mp, xy_mm, xz_mp, xz_mm]
    new_flat = [
        even_rest,
        even_y + odd_y,
        even_y - odd_y,
        even_z + odd_z,
        even_z - odd_z,
        yz_pp,
        yz_mm,
        yz_pm,
        yz_mp,
    ]
    out_ahead = [
        jnp.where(solid, back[BOUNCE[k]], ahead[k] - new_ahead[k]) for k in range(5)
    ]
    out_back = [jnp.where(solid, ahead[BOUNCE[k]], back[k] - new_back[k]) for k in range(5)]
    out_flat = [
        jnp.where(solid, flat[FLAT_OPPOSITE[k]], flat[k] - new_flat[k]) for k in range(9)
    ]
    return out_ahead, out_back, out_flat


def local_frame():
    return lax.rem(lax.axis_index("gx"), 2)


def select_channel(side, k):
    return jnp.where(side == 1, UP[k], DOWN[k])


def scalars(rates_ref, force_ref, side, spread):
    rates = [rates_ref[m] for m in range(19)]
    sixth = 1.0 / 6.0
    sign = jnp.where(side == 1, sixth, -sixth).astype(jnp.float32)
    push = (force_ref[0] * sign, force_ref[1] * sixth, force_ref[2] * sixth)
    cross = tuple(rates[m] * 0.25 for m in (4, 5, 6))
    slots = iter(range(spread.shape[0]))

    def kept(value):
        slot = next(slots)
        spread[slot] = jnp.full(spread.shape[1:], value, jnp.float32)
        return lambda: spread[slot]

    matrices = [
        {place: kept(value) for place, value in matrix.items()}
        for matrix in relaxing_entries(rates)
    ]
    return matrices, tuple(map(kept, cross)), tuple(map(kept, push))


def shift_in_z(halves, step):
    if step == 0:
        return halves
    lane = lax.broadcasted_iota(jnp.int32, halves[0].shape, 1)
    edge = lane == (0 if step > 0 else LANES - 1)
    low, high = (pltpu.roll(value, step % LANES, 1) for value in halves)
    return jnp.where(edge, high, low), jnp.where(edge, low, high)


def relax_tile(load, solid_ref, solid_row, coefficients):
    halves = []
    for lane in range(0, solid_ref.shape[1], LANES):
        solid = solid_ref[pl.ds(solid_row, ROWS), pl.ds(lane, LANES)] == 1
        ahead, back, flat = relax(*load(lane), solid, *coefficients)
        halves.append(ahead + back + flat)
    return list(zip(*halves, strict=True))


OFF, ON, STILL = "off", "on", "still"
GROUP_SIZE = {OFF: 5, ON: 5, STILL: 9}


def wanted(groups, refs):
    first = {OFF: 0, ON: 5, STILL: 10}
    shifts = {OFF: GROUP_SHIFTS, ON: GROUP_SHIFTS, STILL: FLAT_SHIFTS}
    return [
        (first[group] + k, ref, k, shifts[group][k])
        for group, ref in zip(groups, refs, strict=True)
        for k in range(GROUP_SIZE[group])
    ]


def first_kernel(start, rows, groups, f_ref, mask_ref, rates_hbm, force_hbm, *refs):
    *results, f, solid, out, spread, rates, force, sems = refs
    height = mask_ref.shape[0]
    tiles = rows // ROWS + 2
    targets = wanted(groups, results)

    def fetch(i):
        row = (start + (i - 1) * ROWS) % height
        return pltpu.make_async_copy(
            f_ref.at[:, pl.ds(row, ROWS), :], f.at[:, pl.ds(i * ROWS, ROWS), :], sems.at[i]
        )

    small = [
        pltpu.make_async_copy(rates_hbm, rates, sems.at[tiles]),
        pltpu.make_async_copy(force_hbm, force, sems.at[tiles + 1]),
        pltpu.make_async_copy(mask_ref, solid, sems.at[tiles + 2]),
    ]
    for copy in small[:2]:
        copy.start()
    fetch(0).start()
    fetch(1).start()
    small[2].start()
    for i in range(2, tiles):
        fetch(i).start()
    side = local_frame()
    toward = [select_channel(side, k) for k in range(5)]
    away = [select_channel(1 - side, k) for k in range(5)]
    channels = toward + away + list(FLAT)
    for copy in small[:2]:
        copy.wait()
    coefficients = scalars(rates, force, side, spread)

    def collide(i):
        local = i * ROWS
        if i in GROUPS:
            following = [g for g in GROUPS if g > i]
            for j in range(i, min(following[0] if following else tiles, tiles)):
                fetch(j).wait()
        if i == 0:
            small[2].wait()

        def load(lane):
            values = [f[c, pl.ds(local, ROWS), pl.ds(lane, LANES)] for c in channels]
            return values[:5], values[5:10], values[10:]

        row = (start + (i - 1) * ROWS) % height
        pairs = relax_tile(load, solid, row, coefficients)
        for slot, (place, *_) in enumerate(targets):
            for half in range(2):
                out[slot, half, pl.ds(local, ROWS), :] = pairs[place][half]

    def emit(i):
        local = i * ROWS
        row = local - ROWS
        for slot, (_, ref, entry, (step_y, step_z)) in enumerate(targets):
            pair = tuple(out[slot, half, pl.ds(local - step_y, ROWS), :] for half in range(2))
            pair = shift_in_z(pair, step_z)
            for half in range(2):
                ref[entry, pl.ds(row, ROWS), pl.ds(half * LANES, LANES)] = pair[half]

    for i in range(tiles):
        collide(i)
        if i > 1:
            emit(i - 1)


def second_kernel(parts, groups, begin, *refs):
    off_in, refs = refs[: len(parts)], refs[len(parts) :]
    on_in, flat_in, solid, rates, force, *results, spread = refs
    results = results[-len(groups) :]
    coefficients = scalars(rates, force, local_frame(), spread)
    targets = wanted(groups, results)
    for (start, rows), arrived in zip(parts, off_in, strict=True):
        for local in range(0, rows, ROWS):

            def load(lane, local=local, start=start, arrived=arrived):
                own = (pl.ds(local, ROWS), pl.ds(lane, LANES))
                where = (pl.ds(start + local, ROWS), pl.ds(lane, LANES))
                return (
                    [on_in[(k, *where)] for k in range(5)],
                    [arrived[(k, *own)] for k in range(5)],
                    [flat_in[(k, *where)] for k in range(9)],
                )

            pairs = relax_tile(load, solid, start + local, coefficients)
            for place, ref, entry, (_, step_z) in targets:
                pair = shift_in_z(pairs[place], step_z)
                for half in range(2):
                    ref[entry, pl.ds(start - begin + local, ROWS), pl.ds(half * LANES, LANES)] = pair[half]


def place_all(refs, out_ref, moved, sems, number_of, shifts):
    copies = []
    for k, (step, _) in enumerate(shifts):
        both = jnp.concatenate([ref[k] for ref in refs], axis=0)
        moved[k] = pltpu.roll(both, step % both.shape[0], 0) if step else both
        copies.append(pltpu.make_async_copy(moved.at[k], out_ref.at[number_of(k)], sems.at[k]))
        copies[-1].start()
    for copy in copies:
        copy.wait()


def place_flat_kernel(*refs):
    *parts, out_ref, moved, sems = refs
    place_all(parts, out_ref, moved, sems, lambda k: FLAT[k], FLAT_SHIFTS)


def place_on_kernel(*refs):
    *parts, _, out_ref, moved, sems = refs
    side = local_frame()
    place_all(parts, out_ref, moved, sems, lambda k: select_channel(side, k), GROUP_SHIFTS)


def place_off_kernel(p, start, height, *refs):
    *parts, _, out_ref, moved, sems = refs
    side = local_frame()
    own = parts[p]
    rows = own.shape[1]
    first, last = p == 0, start + rows == height
    copies = []

    def send(source, k, to, slot):
        copies.append(
            pltpu.make_async_copy(
                source, out_ref.at[select_channel(1 - side, k), pl.ds(to, source.shape[0]), :], sems.at[slot]
            )
        )
        copies[-1].start()

    slot = 0
    for k, (step, _) in enumerate(GROUP_SHIFTS):
        if step == 0:
            send(own.at[k], k, start, slot)
            slot += 1
    for entry, k in enumerate((1, 2)):
        step = GROUP_SHIFTS[k][0]
        stack = [own[k]]
        if not first:
            stack.insert(0, parts[p - 1][k, pl.ds(parts[p - 1].shape[1] - ROWS, ROWS), :])
        if last:
            stack.append(parts[0][k, pl.ds(0, ROWS), :])
        stack = jnp.concatenate(stack, axis=0)
        size = stack.shape[0]
        moved[entry, pl.ds(0, size), :] = pltpu.roll(stack, step % size, 0)
        begin = start - (0 if first else ROWS)
        low = ROWS if step > 0 else 0
        high = size - (ROWS if step < 0 else 0)
        if last and step > 0:
            send(moved.at[entry, pl.ds(high - ROWS, ROWS), :], k, 0, slot)
            slot += 1
            high -= ROWS
        send(moved.at[entry, pl.ds(low, high - low), :], k, begin + low, slot)
        slot += 1
    for copy in copies:
        copy.wait()


def in_vmem(array):
    return pltpu.with_memory_space_constraint(array, pltpu.VMEM)


def in_hbm(array):
    return pltpu.with_memory_space_constraint(array, pltpu.HBM)


def vmem_result(shape):
    return pltpu.VMEM(shape, jnp.float32)


def hbm_result(shape):
    return pltpu.HBM(shape, jnp.float32)


def params(mebibytes):
    return pltpu.CompilerParams(vmem_limit_bytes=mebibytes << 20)


def in_smem(array):
    return pltpu.with_memory_space_constraint(array, pltpu.SMEM)


def row_parts(height):
    sizes = [height * eighths // 8 for eighths in EIGHTHS]
    assert all(size % ROWS == 0 for size in sizes) and sum(sizes) == height
    return [(sum(sizes[:p]), size) for p, size in enumerate(sizes)]


def on_device(populations, solid_mask, relax_rates, body_force):
    channels, depth, height, breadth = populations.shape
    assert depth == 1 and breadth == 2 * LANES
    count = lax.axis_size("gx")
    assert count % 2 == 0
    off_pairs = [(i, (i + 1) % count if i % 2 else (i - 1) % count) for i in range(count)]
    on_pairs = [(i, i ^ 1) for i in range(count)]
    plane = in_hbm(populations.reshape(channels, height, breadth))
    mask = solid_mask.reshape(height, breadth)
    f32 = jnp.float32
    anywhere = pl.BlockSpec(memory_space=pl.ANY)
    local = pl.BlockSpec(memory_space=pltpu.VMEM)
    small = pl.BlockSpec(memory_space=pltpu.SMEM)
    whole = hbm_result((channels, height, breadth))
    spread = pltpu.VMEM((COEFFICIENTS, ROWS, LANES), f32)

    def cost(rows):
        nodes = rows * breadth
        return pl.CostEstimate(flops=320 * nodes, bytes_accessed=160 * nodes, transcendentals=0)

    def results(groups, rows):
        shapes = tuple(vmem_result((GROUP_SIZE[group], rows, breadth)) for group in groups)
        return shapes, tuple(local for _ in shapes)

    def step_one(start, rows, groups):
        tiles = rows // ROWS + 2
        shapes, specs = results(groups, rows)
        kept = sum(GROUP_SIZE[group] for group in groups)
        return pl.pallas_call(
            functools.partial(first_kernel, start, rows, groups),
            out_shape=shapes,
            in_specs=[anywhere] * 4,
            out_specs=specs,
            scratch_shapes=[
                pltpu.VMEM((channels, tiles * ROWS, breadth), f32),
                pltpu.VMEM((height, breadth), jnp.int32),
                pltpu.VMEM((kept, 2, tiles * ROWS, LANES), f32),
                spread,
                pltpu.SMEM(relax_rates.shape, f32),
                pltpu.SMEM(body_force.shape, f32),
                pltpu.SemaphoreType.DMA((tiles + 3,)),
            ],
            cost_estimate=cost(rows),
            compiler_params=params(8),
        )(plane, in_hbm(mask), in_hbm(relax_rates), in_hbm(body_force))

    def step_two(parts, groups, off, on, flat, carried=None):
        rows = height if carried is not None else sum(rows for _, rows in parts)
        begin = 0 if carried is not None else parts[0][0]
        shapes, specs = results(groups, rows)
        operands = (*off, on, flat, in_vmem(mask), in_smem(relax_rates), in_smem(body_force))
        held = tuple(carried or ())
        return pl.pallas_call(
            functools.partial(second_kernel, parts, groups, begin),
            out_shape=shapes,
            in_specs=[local] * (len(parts) + 3) + [small, small] + [local] * len(held),
            out_specs=specs,
            scratch_shapes=[spread],
            input_output_aliases={len(operands) + i: i for i in range(len(held))},
            cost_estimate=cost(rows),
            compiler_params=params(8),
        )(*operands, *map(in_vmem, held))

    def send(array, pairs):
        return in_vmem(lax.ppermute(array, "gx", pairs))

    parts = row_parts(height)
    offs = []
    for start, rows in parts:
        (off,) = step_one(start, rows, (OFF,))
        offs.append(send(off, off_pairs))
    on, flat = step_one(0, height, (ON, STILL))
    on = send(on, on_pairs)
    arrived, carried = [], ()
    for p, part in enumerate(parts):
        (off,) = step_two([part], (OFF,), [offs[p]], on, flat)
        arrived.append(send(off, off_pairs))
        carried = step_two([part], (ON, STILL), [offs[p]], on, flat, carried)
    on, flat = carried
    on, offs = send(on, on_pairs), arrived

    def place(kernel, groups, result, moved, copies):
        operands = tuple(groups) + ((result,) if result is not None else ())
        return pl.pallas_call(
            kernel,
            out_shape=whole,
            in_specs=[local] * len(groups) + [anywhere] * (result is not None),
            out_specs=anywhere,
            scratch_shapes=[pltpu.VMEM(moved, f32), pltpu.SemaphoreType.DMA((copies,))],
            input_output_aliases={len(groups): 0} if result is not None else {},
            cost_estimate=pl.CostEstimate(
                flops=0, bytes_accessed=20 * height * breadth, transcendentals=0
            ),
            compiler_params=params(4),
        )(*operands)

    result = place(place_flat_kernel, [flat], None, (9, height, breadth), 9)
    for p, (start, rows) in enumerate(parts):
        if p == len(parts) - 1:
            result = place(place_on_kernel, [on], result, (5, height, breadth), 5)
        kernel = functools.partial(place_off_kernel, p, start, height)
        moved = (2, rows + 2 * ROWS, breadth)
        result = place(kernel, offs[: p + 1], result, moved, 6)
    return result.reshape(channels, depth, height, breadth)


def solution(mesh):
    in_specs = (P(None, ("sample", "gx"), None, None), P(("sample", "gx"), None, None), P(), P())
    out_specs = P(None, ("sample", "gx"), None, None)
    return jax.shard_map(
        on_device, mesh=mesh, in_specs=in_specs, out_specs=out_specs, check_vma=False
    )
```

time: 41.6 us -> 43.7 us (1.050)
  starting transfers between devices: 8.29 us -> 4.72 us
  waiting for transfers between devices: 20.3 us -> 23.5 us
  Pallas kernels: 12.7 us -> 15.1 us
    ppermute x8 -> x6, starting transfers between devices: 8.29 us -> 4.72 us  [send(): return in_vmem(lax.ppermute(array, 'gx', pairs))]
    ppermute x8 -> x6, waiting for transfers between devices: 20.3 us -> 23.5 us  [send(): return in_vmem(lax.ppermute(array, 'gx', pairs))]
    pallas_call x7 -> x11, Pallas kernels: 12.7 us -> 15.1 us  [the longest x3 7.12 us: step_one(): pl.pallas_call(functools.partial(first_kernel, start, rows, groups), out_...]
  transfers between devices with their start and end apart: 8 -> 6, of which waited for: 4 -> 4; matrix products, arithmetic and copies ran while one was open for 0% -> 0% of each run, Pallas kernels for 22% -> 23%
where the time goes in v2:
time: 43.7 us; the launch traced here: 43.4 us
  waiting for transfers between devices  23.5 us (54%)
  Pallas kernels  15.1 us (35%)
  starting transfers between devices  4.72 us (11%)
    ppermute x6, waiting for transfers between devices, send(): return in_vmem(lax.ppermute(array, 'gx', pairs))  23.5 us
    pallas_call x3, Pallas kernels, step_one(): pl.pallas_call(functools.partial(first_kernel, start, rows, groups), out_...  7.12 us
    ppermute x6, starting transfers between devices, send(): return in_vmem(lax.ppermute(array, 'gx', pairs))  4.72 us
    pallas_call x4, Pallas kernels, step_two(): pl.pallas_call(functools.partial(second_kernel, parts, groups, begin), ou...  4.46 us
    pallas_call x4, Pallas kernels, place(): pl.pallas_call(kernel, out_shape=whole, in_specs=[local] * len(groups) +...  3.53 us
  transfers between devices with their start and end apart: 6, of which 4 were waited for; matrix products, arithmetic and copies ran while one was open for 0% of the time, Pallas kernels for 23%

profile of v2, /device:TPU:1, one launch (start us, length us, event | category | flops | bytes accessed | tf_op | source)
XLA Modules:
  0.0 43.4 jit_solution(8608646471891422936)
XLA Ops:
  0.0 3.3 %shard_map.47 = (f32[5,128,256]{2,1,0:T(8,128)S(1)}, f32[9,128,256]{2,1,0:T(8,128)S(1)}) custom-call(f32[19,128,256]{2,1,0:T(8,128)} %bitcast.12, s32[128,256]{1,0:T(8,128)} %bitcast.5, f32[19]{0:T(128)} %refs_4_.7, f32[3]{0:T(128)} %refs_5_.7), custom_call_target="tpu_custom_call" | custom-call | flops 10485760 | bytes 5242880 | tf_op jit(solution)/shard_map/pallas_call | solution.py:482
  3.3 0.0 copy-start
  3.3 0.0 copy-start.1
  3.3 0.0 copy-start.2
  3.3 0.1 collective-permute-start.1
  3.4 1.9 %shard_map.46 = f32[5,64,256]{2,1,0:T(8,128)S(1)} custom-call(f32[19,128,256]{2,1,0:T(8,128)} %bitcast.13, s32[128,256]{1,0:T(8,128)} %bitcast.6, f32[19]{0:T(128)} %refs_4_.7, f32[3]{0:T(128)} %refs_5_.7), custom_call_target="tpu_custom_call" | custom-call | flops 5242880 | bytes 2621440 | tf_op jit(solution)/shard_map/pallas_call | solution.py:482
  5.3 2.7 %collective-permute-start = (f32[5,64,256]{2,1,0:T(8,128)S(1)}, f32[5,64,256]{2,1,0:T(8,128)S(1)}, u32[]{:S(2)}, u32[]{:S(2)}) collective-permute-start(f32[5,64,256]{2,1,0:T(8,128)S(1)} %shard_map.46), channel_id=1, source_target_pairs={{0,15},{1,2},{2,1},{3,4},{4,3},{5,6},{6,5},{7,8},{8,7},{9,10},{10,... | collective-permute-start | bytes 983048 | tf_op jit(solution)/shard_map/ppermute | solution.py:518
  8.0 1.9 %shard_map.49 = f32[5,64,256]{2,1,0:T(8,128)S(1)} custom-call(f32[19,128,256]{2,1,0:T(8,128)} %bitcast.14, s32[128,256]{1,0:T(8,128)} %bitcast.7, f32[19]{0:T(128)} %refs_4_.7, f32[3]{0:T(128)} %refs_5_.7), custom_call_target="tpu_custom_call" | custom-call | flops 5242880 | bytes 2621440 | tf_op jit(solution)/shard_map/pallas_call | solution.py:482
  9.9 0.1 collective-permute-start.3
  10.0 9.0 %collective-permute-done.refs_0_ = f32[5,64,256]{2,1,0:T(8,128)S(1)} collective-permute-done((f32[5,64,256]{2,1,0:T(8,128)S(1)}, f32[5,64,256]{2,1,0:T(8,128)S(1)}, u32[]{:S(2)}, u32[]{:S(2)}) %collective-permute-start) | collective-permute-done | bytes 327712 | tf_op jit(solution)/shard_map/ppermute | solution.py:518
  19.0 1.2 %shard_map.51 = (f32[5,128,256]{2,1,0:T(8,128)S(1)}, f32[9,128,256]{2,1,0:T(8,128)S(1)}) custom-call(f32[5,64,256]{2,1,0:T(8,128)S(1)} %collective-permute-done.refs_0_, f32[5,128,256]{2,1,0:T(8,128)S(1)} %collective-permute-done.1.refs_1_, f32[9,128,256]{2,1,0:T(8,128)S(1)} %get-tuple-element.12.refs_2_, s32[128,256]{1,0:T(8,128)S(1)} %bitcast.8, ...), custom_call_target="tpu_custom_call" | custom-call | flops 10485760 | bytes 5242880 | tf_op jit(solution)/shard_map/pallas_call | solution.py:506
  20.3 3.0 %collective-permute-done.3.refs_0_ = f32[5,64,256]{2,1,0:T(8,128)S(1)} collective-permute-done((f32[5,64,256]{2,1,0:T(8,128)S(1)}, f32[5,64,256]{2,1,0:T(8,128)S(1)}, u32[]{:S(2)}, u32[]{:S(2)}) %collective-permute-start.3) | collective-permute-done | bytes 327712 | tf_op jit(solution)/shard_map/ppermute | solution.py:518
  23.3 1.2 %shard_map.52 = (f32[5,128,256]{2,1,0:T(8,128)S(1)}, f32[9,128,256]{2,1,0:T(8,128)S(1)}) custom-call(f32[5,64,256]{2,1,0:T(8,128)S(1)} %collective-permute-done.3.refs_0_, f32[5,128,256]{2,1,0:T(8,128)S(1)} %collective-permute-done.1.refs_1_, f32[9,128,256]{2,1,0:T(8,128)S(1)} %get-tuple-element.12.refs_2_, ...), custom_call_target="tpu_custom_call", output_to_operand_aliasing={{0}: (6, {}), {1}: (7, {})} | custom-call | flops 10485760 | bytes 5242880 | tf_op jit(solution)/shard_map/pallas_call | solution.py:506
  24.5 0.1 collective-permute-start.5
  24.6 1.0 %shard_map.48 = f32[5,64,256]{2,1,0:T(8,128)S(1)} custom-call(f32[5,64,256]{2,1,0:T(8,128)S(1)} %collective-permute-done.refs_0_, f32[5,128,256]{2,1,0:T(8,128)S(1)} %collective-permute-done.1.refs_1_, f32[9,128,256]{2,1,0:T(8,128)S(1)} %get-tuple-element.12.refs_2_, s32[128,256]{1,0:T(8,128)S(1)} %bitcast.10, f32[19]{0:T(128)S(1)} %copy-done.1, f32[3]{0:T(128)S(1)} %copy-done.2), custom_call_target="tpu_custom_call" | custom-call | flops 5242880 | bytes 2621440 | tf_op jit(solution)/shard_map/pallas_call | solution.py:506
  25.6 1.8 %collective-permute-start.2 = (f32[5,64,256]{2,1,0:T(8,128)S(1)}, f32[5,64,256]{2,1,0:T(8,128)S(1)}, u32[]{:S(2)}, u32[]{:S(2)}) collective-permute-start(f32[5,64,256]{2,1,0:T(8,128)S(1)} %shard_map.48), channel_id=1, source_target_pairs={{0,15},{1,2},{2,1},{3,4},{4,3},{5,6},{6,5},{7,8},{8,7},{9,10},{10,... | collective-permute-start | bytes 983048 | tf_op jit(solution)/shard_map/ppermute | solution.py:518
  27.4 1.0 %shard_map.50 = f32[5,64,256]{2,1,0:T(8,128)S(1)} custom-call(f32[5,64,256]{2,1,0:T(8,128)S(1)} %collective-permute-done.3.refs_0_, f32[5,128,256]{2,1,0:T(8,128)S(1)} %collective-permute-done.1.refs_1_, f32[9,128,256]{2,1,0:T(8,128)S(1)} %get-tuple-element.12.refs_2_, s32[128,256]{1,0:T(8,128)S(1)} %bitcast.11, f32[19]{0:T(128)S(1)} %copy-done.1, ...), custom_call_target="tpu_custom_call" | custom-call | flops 5242880 | bytes 2621440 | tf_op jit(solution)/shard_map/pallas_call | solution.py:506
  28.4 0.1 collective-permute-start.4
  28.4 1.1 %shard_map.53.refs_1_ = f32[19,128,256]{2,1,0:T(8,128)} custom-call(f32[9,128,256]{2,1,0:T(8,128)S(1)} %get-tuple-element.16.refs_0_), custom_call_target="tpu_custom_call" | custom-call | bytes 655360 | tf_op jit(solution)/shard_map/pallas_call | solution.py:537
  29.5 8.9 %collective-permute-done.2.refs_0_ = f32[5,64,256]{2,1,0:T(8,128)S(1)} collective-permute-done((f32[5,64,256]{2,1,0:T(8,128)S(1)}, f32[5,64,256]{2,1,0:T(8,128)S(1)}, u32[]{:S(2)}, u32[]{:S(2)}) %collective-permute-start.2) | collective-permute-done | bytes 327712 | tf_op jit(solution)/shard_map/ppermute | solution.py:518
  38.4 0.8 %shard_map.54.refs_1_ = f32[19,128,256]{2,1,0:T(8,128)} custom-call(f32[5,64,256]{2,1,0:T(8,128)S(1)} %collective-permute-done.2.refs_0_, f32[19,128,256]{2,1,0:T(8,128)} %shard_map.53.refs_1_), custom_call_target="tpu_custom_call", output_to_operand_aliasing={{}: (1, {})} | custom-call | bytes 655360 | tf_op jit(solution)/shard_map/pallas_call | solution.py:537
  39.2 0.9 %shard_map.55.refs_2_ = f32[19,128,256]{2,1,0:T(8,128)} custom-call(f32[5,128,256]{2,1,0:T(8,128)S(1)} %collective-permute-done.5.refs_0_, f32[19,128,256]{2,1,0:T(8,128)} %shard_map.54.refs_1_), custom_call_target="tpu_custom_call", output_to_operand_aliasing={{}: (1, {})} | custom-call | bytes 655360 | tf_op jit(solution)/shard_map/pallas_call | solution.py:537
  40.1 2.6 %collective-permute-done.4.refs_1_ = f32[5,64,256]{2,1,0:T(8,128)S(1)} collective-permute-done((f32[5,64,256]{2,1,0:T(8,128)S(1)}, f32[5,64,256]{2,1,0:T(8,128)S(1)}, u32[]{:S(2)}, u32[]{:S(2)}) %collective-permute-start.4) | collective-permute-done | bytes 327712 | tf_op jit(solution)/shard_map/ppermute | solution.py:518
  42.7 0.8 %shard_map.56 = f32[19,128,256]{2,1,0:T(8,128)} custom-call(f32[5,64,256]{2,1,0:T(8,128)S(1)} %collective-permute-done.2.refs_0_, f32[5,64,256]{2,1,0:T(8,128)S(1)} %collective-permute-done.4.refs_1_, f32[19,128,256]{2,1,0:T(8,128)} %shard_map.55.refs_2_), custom_call_target="tpu_custom_call", output_to_operand_aliasing={{}: (2, {})} | custom-call | bytes 655360 | tf_op jit(solution)/shard_map/pallas_call | solution.py:537
  (5 shorter events, 0.0 us)
Async XLA Ops:
  3.3 15.8 %copy-start = (s32[1,128,256]{2,1,0:T(8,128)S(1)}, s32[1,128,256]{2,1,0:T(8,128)}, u32[]{:S(2)}) copy-start(s32[1,128,256]{2,1,0:T(8,128)} %param.5) | copy-start | bytes 393220
  3.3 15.7 %copy-start.1 = (f32[19]{0:T(128)S(1)}, f32[19]{0:T(128)}, u32[]{:S(2)}) copy-start(f32[19]{0:T(128)} %refs_4_.7) | copy-start | bytes 232
  3.3 15.7 %copy-start.2 = (f32[3]{0:T(128)S(1)}, f32[3]{0:T(128)}, u32[]{:S(2)}) copy-start(f32[3]{0:T(128)} %refs_5_.7) | copy-start | bytes 40
  3.3 15.7 %collective-permute-start.1 = (f32[5,128,256]{2,1,0:T(8,128)S(1)}, f32[5,128,256]{2,1,0:T(8,128)S(1)}, u32[]{:S(2)}, u32[]{:S(2)}) collective-permute-start(f32[5,128,256]{2,1,0:T(8,128)S(1)} %get-tuple-element.11), channel_id=1, source_target_pairs={{0,1},{1,0},{2,3},{3,2},{4,5},{5,4},{6,7},{7,6},{8,9},{9,8},{10,11... | collective-permute-start | bytes 1966088 | tf_op jit(solution)/shard_map/ppermute | solution.py:518
  5.3 13.7 %collective-permute-start = (f32[5,64,256]{2,1,0:T(8,128)S(1)}, f32[5,64,256]{2,1,0:T(8,128)S(1)}, u32[]{:S(2)}, u32[]{:S(2)}) collective-permute-start(f32[5,64,256]{2,1,0:T(8,128)S(1)} %shard_map.46), channel_id=1, source_target_pairs={{0,15},{1,2},{2,1},{3,4},{4,3},{5,6},{6,5},{7,8},{8,7},{9,10},{10,... | collective-permute-start | bytes 983048 | tf_op jit(solution)/shard_map/ppermute | solution.py:518
  9.9 13.4 %collective-permute-start.3 = (f32[5,64,256]{2,1,0:T(8,128)S(1)}, f32[5,64,256]{2,1,0:T(8,128)S(1)}, u32[]{:S(2)}, u32[]{:S(2)}) collective-permute-start(f32[5,64,256]{2,1,0:T(8,128)S(1)} %shard_map.49), channel_id=1, source_target_pairs={{0,15},{1,2},{2,1},{3,4},{4,3},{5,6},{6,5},{7,8},{8,7},{9,10},{10,... | collective-permute-start | bytes 983048 | tf_op jit(solution)/shard_map/ppermute | solution.py:518
  24.5 14.7 %collective-permute-start.5 = (f32[5,128,256]{2,1,0:T(8,128)S(1)}, f32[5,128,256]{2,1,0:T(8,128)S(1)}, u32[]{:S(2)}, u32[]{:S(2)}) collective-permute-start(f32[5,128,256]{2,1,0:T(8,128)S(1)} %get-tuple-element.15), channel_id=1, source_target_pairs={{0,1},{1,0},{2,3},{3,2},{4,5},{5,4},{6,7},{7,6},{8,9},{9,8},{10,11... | collective-permute-start | bytes 1966088 | tf_op jit(solution)/shard_map/ppermute | solution.py:518
  25.6 12.8 %collective-permute-start.2 = (f32[5,64,256]{2,1,0:T(8,128)S(1)}, f32[5,64,256]{2,1,0:T(8,128)S(1)}, u32[]{:S(2)}, u32[]{:S(2)}) collective-permute-start(f32[5,64,256]{2,1,0:T(8,128)S(1)} %shard_map.48), channel_id=1, source_target_pairs={{0,15},{1,2},{2,1},{3,4},{4,3},{5,6},{6,5},{7,8},{8,7},{9,10},{10,... | collective-permute-start | bytes 983048 | tf_op jit(solution)/shard_map/ppermute | solution.py:518
  28.4 14.3 %collective-permute-start.4 = (f32[5,64,256]{2,1,0:T(8,128)S(1)}, f32[5,64,256]{2,1,0:T(8,128)S(1)}, u32[]{:S(2)}, u32[]{:S(2)}) collective-permute-start(f32[5,64,256]{2,1,0:T(8,128)S(1)} %shard_map.50), channel_id=1, source_target_pairs={{0,15},{1,2},{2,1},{3,4},{4,3},{5,6},{6,5},{7,8},{8,7},{9,10},{10,... | collective-permute-start | bytes 983048 | tf_op jit(solution)/shard_map/ppermute | solution.py:518

commit v3 on v2

--- a/solution.py
+++ b/solution.py
@@ -10,7 +10,7 @@
 
 EIGHTHS = (4, 4)
 COEFFICIENTS = 52
-GROUPS = (0, 2, 5)
+GROUPS = (0, 1, 3, 6, 10)
 LANES = 128
 ROWS = 8
 
@@ -269,6 +269,9 @@
     height = mask_ref.shape[0]
     tiles = rows // ROWS + 2
     targets = wanted(groups, results)
+    closed = rows == height
+    collided = range(1, tiles - 1) if closed else range(tiles)
+    copied = {1: tiles - 1, tiles - 2: 0} if closed else {}
 
     def fetch(i):
         row = (start + (i - 1) * ROWS) % height
@@ -283,11 +286,10 @@
     ]
     for copy in small[:2]:
         copy.start()
-    fetch(0).start()
-    fetch(1).start()
-    small[2].start()
-    for i in range(2, tiles):
+    for i in collided:
         fetch(i).start()
+        if i == 1:
+            small[2].start()
     side = local_frame()
     toward = [select_channel(side, k) for k in range(5)]
     away = [select_channel(1 - side, k) for k in range(5)]
@@ -299,10 +301,10 @@
     def collide(i):
         local = i * ROWS
         if i in GROUPS:
-            following = [g for g in GROUPS if g > i]
-            for j in range(i, min(following[0] if following else tiles, tiles)):
+            end = min((g for g in GROUPS if g > i), default=tiles)
+            for j in range(i, min(end, collided[-1] + 1)):
                 fetch(j).wait()
-        if i == 0:
+        if i == collided[0]:
             small[2].wait()
 
         def load(lane):
@@ -314,6 +316,8 @@
         for slot, (place, *_) in enumerate(targets):
             for half in range(2):
                 out[slot, half, pl.ds(local, ROWS), :] = pairs[place][half]
+                if i in copied:
+                    out[slot, half, pl.ds(copied[i] * ROWS, ROWS), :] = pairs[place][half]
 
     def emit(i):
         local = i * ROWS
@@ -324,10 +328,13 @@
             for half in range(2):
                 ref[entry, pl.ds(row, ROWS), pl.ds(half * LANES, LANES)] = pair[half]
 
-    for i in range(tiles):
+    for i in collided:
         collide(i)
-        if i > 1:
+        if i >= collided[0] + 2:
             emit(i - 1)
+    if closed:
+        emit(tiles - 2)
+        emit(1)
 
 
 def second_kernel(parts, groups, begin, *refs):
@@ -393,11 +400,7 @@
         )
         copies[-1].start()
 
-    slot = 0
-    for k, (step, _) in enumerate(GROUP_SHIFTS):
-        if step == 0:
-            send(own.at[k], k, start, slot)
-            slot += 1
+    slot = 3
     for entry, k in enumerate((1, 2)):
         step = GROUP_SHIFTS[k][0]
         stack = [own[k]]
@@ -417,6 +420,8 @@
             high -= ROWS
         send(moved.at[entry, pl.ds(low, high - low), :], k, begin + low, slot)
         slot += 1
+    for slot, k in enumerate((0, 3, 4)):
+        send(own.at[k], k, start, slot)
     for copy in copies:
         copy.wait()
 

time: 43.7 us -> 43.3 us (level)
  no operation moved by 1% of the time
where the time goes in v3:
time: 43.3 us; the launch traced here: 43.1 us
  waiting for transfers between devices  23.5 us (54%)
  Pallas kernels  14.7 us (34%)
  starting transfers between devices  4.72 us (11%)
    ppermute x6, waiting for transfers between devices, send(): return in_vmem(lax.ppermute(array, 'gx', pairs))  23.5 us
    pallas_call x3, Pallas kernels, step_one(): pl.pallas_call(functools.partial(first_kernel, start, rows, groups), out_...  6.75 us
    ppermute x6, starting transfers between devices, send(): return in_vmem(lax.ppermute(array, 'gx', pairs))  4.72 us
    pallas_call x4, Pallas kernels, step_two(): pl.pallas_call(functools.partial(second_kernel, parts, groups, begin), ou...  4.46 us
    pallas_call x4, Pallas kernels, place(): pl.pallas_call(kernel, out_shape=whole, in_specs=[local] * len(groups) +...  3.53 us
  transfers between devices with their start and end apart: 6, of which 4 were waited for; matrix products, arithmetic and copies ran while one was open for 0% of the time, Pallas kernels for 23%

profile of v3, /device:TPU:1, one launch (start us, length us, event | category | flops | bytes accessed | tf_op | source)
XLA Modules:
  0.0 43.1 jit_solution(9637027103861063213)
XLA Ops:
  0.0 2.9 %shard_map.47 = (f32[5,128,256]{2,1,0:T(8,128)S(1)}, f32[9,128,256]{2,1,0:T(8,128)S(1)}) custom-call(f32[19,128,256]{2,1,0:T(8,128)} %bitcast.12, s32[128,256]{1,0:T(8,128)} %bitcast.5, f32[19]{0:T(128)} %refs_4_.7, f32[3]{0:T(128)} %refs_5_.7), custom_call_target="tpu_custom_call" | custom-call | flops 10485760 | bytes 5242880 | tf_op jit(solution)/shard_map/pallas_call | solution.py:487
  2.9 0.0 copy-start
  3.0 0.0 copy-start.1
  3.0 0.0 copy-start.2
  3.0 0.1 collective-permute-start.1
  3.1 1.9 %shard_map.46 = f32[5,64,256]{2,1,0:T(8,128)S(1)} custom-call(f32[19,128,256]{2,1,0:T(8,128)} %bitcast.13, s32[128,256]{1,0:T(8,128)} %bitcast.6, f32[19]{0:T(128)} %refs_4_.7, f32[3]{0:T(128)} %refs_5_.7), custom_call_target="tpu_custom_call" | custom-call | flops 5242880 | bytes 2621440 | tf_op jit(solution)/shard_map/pallas_call | solution.py:487
  5.0 2.7 %collective-permute-start = (f32[5,64,256]{2,1,0:T(8,128)S(1)}, f32[5,64,256]{2,1,0:T(8,128)S(1)}, u32[]{:S(2)}, u32[]{:S(2)}) collective-permute-start(f32[5,64,256]{2,1,0:T(8,128)S(1)} %shard_map.46), channel_id=1, source_target_pairs={{0,15},{1,2},{2,1},{3,4},{4,3},{5,6},{6,5},{7,8},{8,7},{9,10},{10,... | collective-permute-start | bytes 983048 | tf_op jit(solution)/shard_map/ppermute | solution.py:523
  7.6 1.9 %shard_map.49 = f32[5,64,256]{2,1,0:T(8,128)S(1)} custom-call(f32[19,128,256]{2,1,0:T(8,128)} %bitcast.14, s32[128,256]{1,0:T(8,128)} %bitcast.7, f32[19]{0:T(128)} %refs_4_.7, f32[3]{0:T(128)} %refs_5_.7), custom_call_target="tpu_custom_call" | custom-call | flops 5242880 | bytes 2621440 | tf_op jit(solution)/shard_map/pallas_call | solution.py:487
  9.6 0.1 collective-permute-start.3
  9.6 9.0 %collective-permute-done.refs_0_ = f32[5,64,256]{2,1,0:T(8,128)S(1)} collective-permute-done((f32[5,64,256]{2,1,0:T(8,128)S(1)}, f32[5,64,256]{2,1,0:T(8,128)S(1)}, u32[]{:S(2)}, u32[]{:S(2)}) %collective-permute-start) | collective-permute-done | bytes 327712 | tf_op jit(solution)/shard_map/ppermute | solution.py:523
  18.7 1.2 %shard_map.51 = (f32[5,128,256]{2,1,0:T(8,128)S(1)}, f32[9,128,256]{2,1,0:T(8,128)S(1)}) custom-call(f32[5,64,256]{2,1,0:T(8,128)S(1)} %collective-permute-done.refs_0_, f32[5,128,256]{2,1,0:T(8,128)S(1)} %collective-permute-done.1.refs_1_, f32[9,128,256]{2,1,0:T(8,128)S(1)} %get-tuple-element.12.refs_2_, s32[128,256]{1,0:T(8,128)S(1)} %bitcast.8, ...), custom_call_target="tpu_custom_call" | custom-call | flops 10485760 | bytes 5242880 | tf_op jit(solution)/shard_map/pallas_call | solution.py:511
  19.9 3.0 %collective-permute-done.3.refs_0_ = f32[5,64,256]{2,1,0:T(8,128)S(1)} collective-permute-done((f32[5,64,256]{2,1,0:T(8,128)S(1)}, f32[5,64,256]{2,1,0:T(8,128)S(1)}, u32[]{:S(2)}, u32[]{:S(2)}) %collective-permute-start.3) | collective-permute-done | bytes 327712 | tf_op jit(solution)/shard_map/ppermute | solution.py:523
  22.9 1.2 %shard_map.52 = (f32[5,128,256]{2,1,0:T(8,128)S(1)}, f32[9,128,256]{2,1,0:T(8,128)S(1)}) custom-call(f32[5,64,256]{2,1,0:T(8,128)S(1)} %collective-permute-done.3.refs_0_, f32[5,128,256]{2,1,0:T(8,128)S(1)} %collective-permute-done.1.refs_1_, f32[9,128,256]{2,1,0:T(8,128)S(1)} %get-tuple-element.12.refs_2_, ...), custom_call_target="tpu_custom_call", output_to_operand_aliasing={{0}: (6, {}), {1}: (7, {})} | custom-call | flops 10485760 | bytes 5242880 | tf_op jit(solution)/shard_map/pallas_call | solution.py:511
  24.2 0.1 collective-permute-start.5
  24.3 1.0 %shard_map.48 = f32[5,64,256]{2,1,0:T(8,128)S(1)} custom-call(f32[5,64,256]{2,1,0:T(8,128)S(1)} %collective-permute-done.refs_0_, f32[5,128,256]{2,1,0:T(8,128)S(1)} %collective-permute-done.1.refs_1_, f32[9,128,256]{2,1,0:T(8,128)S(1)} %get-tuple-element.12.refs_2_, s32[128,256]{1,0:T(8,128)S(1)} %bitcast.10, f32[19]{0:T(128)S(1)} %copy-done.1, f32[3]{0:T(128)S(1)} %copy-done.2), custom_call_target="tpu_custom_call" | custom-call | flops 5242880 | bytes 2621440 | tf_op jit(solution)/shard_map/pallas_call | solution.py:511
  25.2 1.8 %collective-permute-start.2 = (f32[5,64,256]{2,1,0:T(8,128)S(1)}, f32[5,64,256]{2,1,0:T(8,128)S(1)}, u32[]{:S(2)}, u32[]{:S(2)}) collective-permute-start(f32[5,64,256]{2,1,0:T(8,128)S(1)} %shard_map.48), channel_id=1, source_target_pairs={{0,15},{1,2},{2,1},{3,4},{4,3},{5,6},{6,5},{7,8},{8,7},{9,10},{10,... | collective-permute-start | bytes 983048 | tf_op jit(solution)/shard_map/ppermute | solution.py:523
  27.0 1.0 %shard_map.50 = f32[5,64,256]{2,1,0:T(8,128)S(1)} custom-call(f32[5,64,256]{2,1,0:T(8,128)S(1)} %collective-permute-done.3.refs_0_, f32[5,128,256]{2,1,0:T(8,128)S(1)} %collective-permute-done.1.refs_1_, f32[9,128,256]{2,1,0:T(8,128)S(1)} %get-tuple-element.12.refs_2_, s32[128,256]{1,0:T(8,128)S(1)} %bitcast.11, f32[19]{0:T(128)S(1)} %copy-done.1, ...), custom_call_target="tpu_custom_call" | custom-call | flops 5242880 | bytes 2621440 | tf_op jit(solution)/shard_map/pallas_call | solution.py:511
  28.0 0.1 collective-permute-start.4
  28.1 1.1 %shard_map.53.refs_1_ = f32[19,128,256]{2,1,0:T(8,128)} custom-call(f32[9,128,256]{2,1,0:T(8,128)S(1)} %get-tuple-element.16.refs_0_), custom_call_target="tpu_custom_call" | custom-call | bytes 655360 | tf_op jit(solution)/shard_map/pallas_call | solution.py:542
  29.2 8.9 %collective-permute-done.2.refs_0_ = f32[5,64,256]{2,1,0:T(8,128)S(1)} collective-permute-done((f32[5,64,256]{2,1,0:T(8,128)S(1)}, f32[5,64,256]{2,1,0:T(8,128)S(1)}, u32[]{:S(2)}, u32[]{:S(2)}) %collective-permute-start.2) | collective-permute-done | bytes 327712 | tf_op jit(solution)/shard_map/ppermute | solution.py:523
  38.1 0.8 %shard_map.54.refs_1_ = f32[19,128,256]{2,1,0:T(8,128)} custom-call(f32[5,64,256]{2,1,0:T(8,128)S(1)} %collective-permute-done.2.refs_0_, f32[19,128,256]{2,1,0:T(8,128)} %shard_map.53.refs_1_), custom_call_target="tpu_custom_call", output_to_operand_aliasing={{}: (1, {})} | custom-call | bytes 655360 | tf_op jit(solution)/shard_map/pallas_call | solution.py:542
  38.9 0.9 %shard_map.55.refs_2_ = f32[19,128,256]{2,1,0:T(8,128)} custom-call(f32[5,128,256]{2,1,0:T(8,128)S(1)} %collective-permute-done.5.refs_0_, f32[19,128,256]{2,1,0:T(8,128)} %shard_map.54.refs_1_), custom_call_target="tpu_custom_call", output_to_operand_aliasing={{}: (1, {})} | custom-call | bytes 655360 | tf_op jit(solution)/shard_map/pallas_call | solution.py:542
  39.8 2.6 %collective-permute-done.4.refs_1_ = f32[5,64,256]{2,1,0:T(8,128)S(1)} collective-permute-done((f32[5,64,256]{2,1,0:T(8,128)S(1)}, f32[5,64,256]{2,1,0:T(8,128)S(1)}, u32[]{:S(2)}, u32[]{:S(2)}) %collective-permute-start.4) | collective-permute-done | bytes 327712 | tf_op jit(solution)/shard_map/ppermute | solution.py:523
  42.3 0.8 %shard_map.56 = f32[19,128,256]{2,1,0:T(8,128)} custom-call(f32[5,64,256]{2,1,0:T(8,128)S(1)} %collective-permute-done.2.refs_0_, f32[5,64,256]{2,1,0:T(8,128)S(1)} %collective-permute-done.4.refs_1_, f32[19,128,256]{2,1,0:T(8,128)} %shard_map.55.refs_2_), custom_call_target="tpu_custom_call", output_to_operand_aliasing={{}: (2, {})} | custom-call | bytes 655360 | tf_op jit(solution)/shard_map/pallas_call | solution.py:542
  (5 shorter events, 0.0 us)
Async XLA Ops:
  2.9 15.7 %copy-start = (s32[1,128,256]{2,1,0:T(8,128)S(1)}, s32[1,128,256]{2,1,0:T(8,128)}, u32[]{:S(2)}) copy-start(s32[1,128,256]{2,1,0:T(8,128)} %param.5) | copy-start | bytes 393220
  3.0 15.7 %copy-start.1 = (f32[19]{0:T(128)S(1)}, f32[19]{0:T(128)}, u32[]{:S(2)}) copy-start(f32[19]{0:T(128)} %refs_4_.7) | copy-start | bytes 232
  3.0 15.7 %copy-start.2 = (f32[3]{0:T(128)S(1)}, f32[3]{0:T(128)}, u32[]{:S(2)}) copy-start(f32[3]{0:T(128)} %refs_5_.7) | copy-start | bytes 40
  3.0 15.7 %collective-permute-start.1 = (f32[5,128,256]{2,1,0:T(8,128)S(1)}, f32[5,128,256]{2,1,0:T(8,128)S(1)}, u32[]{:S(2)}, u32[]{:S(2)}) collective-permute-start(f32[5,128,256]{2,1,0:T(8,128)S(1)} %get-tuple-element.11), channel_id=1, source_target_pairs={{0,1},{1,0},{2,3},{3,2},{4,5},{5,4},{6,7},{7,6},{8,9},{9,8},{10,11... | collective-permute-start | bytes 1966088 | tf_op jit(solution)/shard_map/ppermute | solution.py:523
  5.0 13.7 %collective-permute-start = (f32[5,64,256]{2,1,0:T(8,128)S(1)}, f32[5,64,256]{2,1,0:T(8,128)S(1)}, u32[]{:S(2)}, u32[]{:S(2)}) collective-permute-start(f32[5,64,256]{2,1,0:T(8,128)S(1)} %shard_map.46), channel_id=1, source_target_pairs={{0,15},{1,2},{2,1},{3,4},{4,3},{5,6},{6,5},{7,8},{8,7},{9,10},{10,... | collective-permute-start | bytes 983048 | tf_op jit(solution)/shard_map/ppermute | solution.py:523
  9.6 13.4 %collective-permute-start.3 = (f32[5,64,256]{2,1,0:T(8,128)S(1)}, f32[5,64,256]{2,1,0:T(8,128)S(1)}, u32[]{:S(2)}, u32[]{:S(2)}) collective-permute-start(f32[5,64,256]{2,1,0:T(8,128)S(1)} %shard_map.49), channel_id=1, source_target_pairs={{0,15},{1,2},{2,1},{3,4},{4,3},{5,6},{6,5},{7,8},{8,7},{9,10},{10,... | collective-permute-start | bytes 983048 | tf_op jit(solution)/shard_map/ppermute | solution.py:523
  24.2 14.7 %collective-permute-start.5 = (f32[5,128,256]{2,1,0:T(8,128)S(1)}, f32[5,128,256]{2,1,0:T(8,128)S(1)}, u32[]{:S(2)}, u32[]{:S(2)}) collective-permute-start(f32[5,128,256]{2,1,0:T(8,128)S(1)} %get-tuple-element.15), channel_id=1, source_target_pairs={{0,1},{1,0},{2,3},{3,2},{4,5},{5,4},{6,7},{7,6},{8,9},{9,8},{10,11... | collective-permute-start | bytes 1966088 | tf_op jit(solution)/shard_map/ppermute | solution.py:523
  25.2 12.8 %collective-permute-start.2 = (f32[5,64,256]{2,1,0:T(8,128)S(1)}, f32[5,64,256]{2,1,0:T(8,128)S(1)}, u32[]{:S(2)}, u32[]{:S(2)}) collective-permute-start(f32[5,64,256]{2,1,0:T(8,128)S(1)} %shard_map.48), channel_id=1, source_target_pairs={{0,15},{1,2},{2,1},{3,4},{4,3},{5,6},{6,5},{7,8},{8,7},{9,10},{10,... | collective-permute-start | bytes 983048 | tf_op jit(solution)/shard_map/ppermute | solution.py:523
  28.0 14.3 %collective-permute-start.4 = (f32[5,64,256]{2,1,0:T(8,128)S(1)}, f32[5,64,256]{2,1,0:T(8,128)S(1)}, u32[]{:S(2)}, u32[]{:S(2)}) collective-permute-start(f32[5,64,256]{2,1,0:T(8,128)S(1)} %shard_map.50), channel_id=1, source_target_pairs={{0,15},{1,2},{2,1},{3,4},{4,3},{5,6},{6,5},{7,8},{8,7},{9,10},{10,... | collective-permute-start | bytes 983048 | tf_op jit(solution)/shard_map/ppermute | solution.py:523

commit v4 on v3

--- a/solution.py
+++ b/solution.py
@@ -232,6 +232,17 @@
     return matrices, tuple(map(kept, cross)), tuple(map(kept, push))
 
 
+def kept_scalars(spread):
+    slots = iter(range(spread.shape[0]))
+
+    def kept():
+        slot = next(slots)
+        return lambda: spread[slot]
+
+    matrices = [{place: kept() for place in matrix} for matrix in relaxing_entries([1.0] * 19)]
+    return matrices, tuple(kept() for _ in range(3)), tuple(kept() for _ in range(3))
+
+
 def shift_in_z(halves, step):
     if step == 0:
         return halves
@@ -264,8 +275,11 @@
     ]
 
 
-def first_kernel(start, rows, groups, f_ref, mask_ref, rates_hbm, force_hbm, *refs):
-    *results, f, solid, out, spread, rates, force, sems = refs
+def first_kernel(start, rows, groups, share, f_ref, mask_ref, rates_hbm, force_hbm, *refs):
+    if share:
+        *results, spread, f, solid, out, rates, force, sems = refs
+    else:
+        *results, f, solid, out, spread, rates, force, sems = refs
     height = mask_ref.shape[0]
     tiles = rows // ROWS + 2
     targets = wanted(groups, results)
@@ -339,9 +353,9 @@
 
 def second_kernel(parts, groups, begin, *refs):
     off_in, refs = refs[: len(parts)], refs[len(parts) :]
-    on_in, flat_in, solid, rates, force, *results, spread = refs
+    on_in, flat_in, solid, spread, *results = refs
     results = results[-len(groups) :]
-    coefficients = scalars(rates, force, local_frame(), spread)
+    coefficients = kept_scalars(spread)
     targets = wanted(groups, results)
     for (start, rows), arrived in zip(parts, off_in, strict=True):
         for local in range(0, rows, ROWS):
@@ -446,10 +460,6 @@
     return pltpu.CompilerParams(vmem_limit_bytes=mebibytes << 20)
 
 
-def in_smem(array):
-    return pltpu.with_memory_space_constraint(array, pltpu.SMEM)
-
-
 def row_parts(height):
     sizes = [height * eighths // 8 for eighths in EIGHTHS]
     assert all(size % ROWS == 0 for size in sizes) and sum(sizes) == height
@@ -480,12 +490,14 @@
         shapes = tuple(vmem_result((GROUP_SIZE[group], rows, breadth)) for group in groups)
         return shapes, tuple(local for _ in shapes)
 
-    def step_one(start, rows, groups):
+    def step_one(start, rows, groups, share=False):
         tiles = rows // ROWS + 2
         shapes, specs = results(groups, rows)
         kept = sum(GROUP_SIZE[group] for group in groups)
+        if share:
+            shapes, specs = shapes + (vmem_result(spread.shape),), specs + (local,)
         return pl.pallas_call(
-            functools.partial(first_kernel, start, rows, groups),
+            functools.partial(first_kernel, start, rows, groups, share),
             out_shape=shapes,
             in_specs=[anywhere] * 4,
             out_specs=specs,
@@ -493,7 +505,7 @@
                 pltpu.VMEM((channels, tiles * ROWS, breadth), f32),
                 pltpu.VMEM((height, breadth), jnp.int32),
                 pltpu.VMEM((kept, 2, tiles * ROWS, LANES), f32),
-                spread,
+                *(() if share else (spread,)),
                 pltpu.SMEM(relax_rates.shape, f32),
                 pltpu.SMEM(body_force.shape, f32),
                 pltpu.SemaphoreType.DMA((tiles + 3,)),
@@ -506,14 +518,13 @@
         rows = height if carried is not None else sum(rows for _, rows in parts)
         begin = 0 if carried is not None else parts[0][0]
         shapes, specs = results(groups, rows)
-        operands = (*off, on, flat, in_vmem(mask), in_smem(relax_rates), in_smem(body_force))
+        operands = (*off, on, flat, in_vmem(mask), shared)
         held = tuple(carried or ())
         return pl.pallas_call(
             functools.partial(second_kernel, parts, groups, begin),
             out_shape=shapes,
-            in_specs=[local] * (len(parts) + 3) + [small, small] + [local] * len(held),
+            in_specs=[local] * (len(parts) + 4 + len(held)),
             out_specs=specs,
-            scratch_shapes=[spread],
             input_output_aliases={len(operands) + i: i for i in range(len(held))},
             cost_estimate=cost(rows),
             compiler_params=params(8),
@@ -523,9 +534,10 @@
         return in_vmem(lax.ppermute(array, "gx", pairs))
 
     parts = row_parts(height)
-    offs = []
-    for start, rows in parts:
-        (off,) = step_one(start, rows, (OFF,))
+    offs, shared = [], None
+    for p, (start, rows) in enumerate(parts):
+        off, *extra = step_one(start, rows, (OFF,), share=p == 0)
+        shared = extra[0] if p == 0 else shared
         offs.append(send(off, off_pairs))
     on, flat = step_one(0, height, (ON, STILL))
     on = send(on, on_pairs)

time: 43.3 us -> 42.1 us (0.972)
  Pallas kernels: 14.7 us -> 12.5 us
  waiting for transfers between devices: 23.5 us -> 24.7 us
    pallas_call x4, Pallas kernels: 4.46 us -> 2.2 us  [step_two(): pl.pallas_call(functools.partial(second_kernel, parts, groups, begin), ou...]
    ppermute x6, waiting for transfers between devices: 23.5 us -> 24.7 us  [send(): return in_vmem(lax.ppermute(array, 'gx', pairs))]
  transfers between devices with their start and end apart: 6 -> 6, of which waited for: 4 -> 4; matrix products, arithmetic and copies ran while one was open for 0% -> 0% of each run, Pallas kernels for 23% -> 19%
where the time goes in v4:
time: 42.1 us; the launch traced here: 41.9 us
  waiting for transfers between devices  24.7 us (59%)
  Pallas kernels  12.5 us (30%)
  starting transfers between devices  4.72 us (11%)
    ppermute x6, waiting for transfers between devices, send(): return in_vmem(lax.ppermute(array, 'gx', pairs))  24.7 us
    pallas_call x3, Pallas kernels, step_one(): pl.pallas_call(functools.partial(first_kernel, start, rows, groups, share...  6.75 us
    ppermute x6, starting transfers between devices, send(): return in_vmem(lax.ppermute(array, 'gx', pairs))  4.72 us
    pallas_call x4, Pallas kernels, place(): pl.pallas_call(kernel, out_shape=whole, in_specs=[local] * len(groups) +...  3.53 us
    pallas_call x4, Pallas kernels, step_two(): pl.pallas_call(functools.partial(second_kernel, parts, groups, begin), ou...  2.2 us
  transfers between devices with their start and end apart: 6, of which 4 were waited for; matrix products, arithmetic and copies ran while one was open for 0% of the time, Pallas kernels for 19%

profile of v4, /device:TPU:1, one launch (start us, length us, event | category | flops | bytes accessed | tf_op | source)
XLA Modules:
  0.0 41.9 jit_solution(16134393059568560911)
XLA Ops:
  0.0 2.9 %shard_map.47 = (f32[5,128,256]{2,1,0:T(8,128)S(1)}, f32[9,128,256]{2,1,0:T(8,128)S(1)}) custom-call(f32[19,128,256]{2,1,0:T(8,128)} %bitcast.12, s32[128,256]{1,0:T(8,128)} %bitcast.5, f32[19]{0:T(128)} %rates_hbm.5, f32[3]{0:T(128)} %force_hbm.5), custom_call_target="tpu_custom_call" | custom-call | flops 10485760 | bytes 5242880 | tf_op jit(solution)/shard_map/pallas_call | solution.py:499
  2.9 0.0 copy-start
  3.0 0.1 collective-permute-start.1
  3.0 1.9 %shard_map.46 = (f32[5,64,256]{2,1,0:T(8,128)S(1)}, f32[52,8,128]{2,1,0:T(8,128)S(1)}) custom-call(f32[19,128,256]{2,1,0:T(8,128)} %bitcast.13, s32[128,256]{1,0:T(8,128)} %bitcast.6, f32[19]{0:T(128)} %rates_hbm.5, f32[3]{0:T(128)} %force_hbm.5), custom_call_target="tpu_custom_call" | custom-call | flops 5242880 | bytes 2621440 | tf_op jit(solution)/shard_map/pallas_call | solution.py:499
  5.0 2.7 %collective-permute-start = (f32[5,64,256]{2,1,0:T(8,128)S(1)}, f32[5,64,256]{2,1,0:T(8,128)S(1)}, u32[]{:S(2)}, u32[]{:S(2)}) collective-permute-start(f32[5,64,256]{2,1,0:T(8,128)S(1)} %get-tuple-element.13), channel_id=1, source_target_pairs={{0,15},{1,2},{2,1},{3,4},{4,3},{5,6},{6,5},{7,8},{8,7},{9,10},{10,... | collective-permute-start | bytes 983048 | tf_op jit(solution)/shard_map/ppermute | solution.py:534
  7.6 1.9 %shard_map.49 = f32[5,64,256]{2,1,0:T(8,128)S(1)} custom-call(f32[19,128,256]{2,1,0:T(8,128)} %bitcast.14, s32[128,256]{1,0:T(8,128)} %bitcast.7, f32[19]{0:T(128)} %rates_hbm.5, f32[3]{0:T(128)} %force_hbm.5), custom_call_target="tpu_custom_call" | custom-call | flops 5242880 | bytes 2621440 | tf_op jit(solution)/shard_map/pallas_call | solution.py:499
  9.5 0.1 collective-permute-start.3
  9.6 9.0 %collective-permute-done.refs_0_ = f32[5,64,256]{2,1,0:T(8,128)S(1)} collective-permute-done((f32[5,64,256]{2,1,0:T(8,128)S(1)}, f32[5,64,256]{2,1,0:T(8,128)S(1)}, u32[]{:S(2)}, u32[]{:S(2)}) %collective-permute-start) | collective-permute-done | bytes 327712 | tf_op jit(solution)/shard_map/ppermute | solution.py:534
  18.7 0.0 collective-permute-done.1.refs_1_
  18.7 0.7 %shard_map.51 = (f32[5,128,256]{2,1,0:T(8,128)S(1)}, f32[9,128,256]{2,1,0:T(8,128)S(1)}) custom-call(f32[5,64,256]{2,1,0:T(8,128)S(1)} %collective-permute-done.refs_0_, f32[5,128,256]{2,1,0:T(8,128)S(1)} %collective-permute-done.1.refs_1_, f32[9,128,256]{2,1,0:T(8,128)S(1)} %get-tuple-element.15.refs_2_, s32[128,256]{1,0:T(8,128)S(1)} %bitcast.8, ...), custom_call_target="tpu_custom_call" | custom-call | flops 10485760 | bytes 5242880 | tf_op jit(solution)/shard_map/pallas_call | solution.py:523
  19.3 3.6 %collective-permute-done.3.refs_0_ = f32[5,64,256]{2,1,0:T(8,128)S(1)} collective-permute-done((f32[5,64,256]{2,1,0:T(8,128)S(1)}, f32[5,64,256]{2,1,0:T(8,128)S(1)}, u32[]{:S(2)}, u32[]{:S(2)}) %collective-permute-start.3) | collective-permute-done | bytes 327712 | tf_op jit(solution)/shard_map/ppermute | solution.py:534
  22.9 0.7 %shard_map.52 = (f32[5,128,256]{2,1,0:T(8,128)S(1)}, f32[9,128,256]{2,1,0:T(8,128)S(1)}) custom-call(f32[5,64,256]{2,1,0:T(8,128)S(1)} %collective-permute-done.3.refs_0_, f32[5,128,256]{2,1,0:T(8,128)S(1)} %collective-permute-done.1.refs_1_, f32[9,128,256]{2,1,0:T(8,128)S(1)} %get-tuple-element.15.refs_2_, ...), custom_call_target="tpu_custom_call", output_to_operand_aliasing={{0}: (5, {}), {1}: (6, {})} | custom-call | flops 10485760 | bytes 5242880 | tf_op jit(solution)/shard_map/pallas_call | solution.py:523
  23.6 0.1 collective-permute-start.5
  23.7 0.4 %shard_map.48 = f32[5,64,256]{2,1,0:T(8,128)S(1)} custom-call(f32[5,64,256]{2,1,0:T(8,128)S(1)} %collective-permute-done.refs_0_, f32[5,128,256]{2,1,0:T(8,128)S(1)} %collective-permute-done.1.refs_1_, f32[9,128,256]{2,1,0:T(8,128)S(1)} %get-tuple-element.15.refs_2_, s32[128,256]{1,0:T(8,128)S(1)} %bitcast.10, f32[52,8,128]{2,1,0:T(8,128)S(1)} %get-tuple-element.16.refs_4_), custom_call_target="tpu_custom_call" | custom-call | flops 5242880 | bytes 2621440 | tf_op jit(solution)/shard_map/pallas_call | solution.py:523
  24.1 1.8 %collective-permute-start.2 = (f32[5,64,256]{2,1,0:T(8,128)S(1)}, f32[5,64,256]{2,1,0:T(8,128)S(1)}, u32[]{:S(2)}, u32[]{:S(2)}) collective-permute-start(f32[5,64,256]{2,1,0:T(8,128)S(1)} %shard_map.48), channel_id=1, source_target_pairs={{0,15},{1,2},{2,1},{3,4},{4,3},{5,6},{6,5},{7,8},{8,7},{9,10},{10,... | collective-permute-start | bytes 983048 | tf_op jit(solution)/shard_map/ppermute | solution.py:534
  25.9 0.4 %shard_map.50 = f32[5,64,256]{2,1,0:T(8,128)S(1)} custom-call(f32[5,64,256]{2,1,0:T(8,128)S(1)} %collective-permute-done.3.refs_0_, f32[5,128,256]{2,1,0:T(8,128)S(1)} %collective-permute-done.1.refs_1_, f32[9,128,256]{2,1,0:T(8,128)S(1)} %get-tuple-element.15.refs_2_, s32[128,256]{1,0:T(8,128)S(1)} %bitcast.11, f32[52,8,128]{2,1,0:T(8,128)S(1)} %get-tuple-element.16.refs_4_), custom_call_target="tpu_custom_call" | custom-call | flops 5242880 | bytes 2621440 | tf_op jit(solution)/shard_map/pallas_call | solution.py:523
  26.3 0.0 collective-permute-start.4
  26.3 1.1 %shard_map.53.refs_1_ = f32[19,128,256]{2,1,0:T(8,128)} custom-call(f32[9,128,256]{2,1,0:T(8,128)S(1)} %get-tuple-element.20.refs_0_), custom_call_target="tpu_custom_call" | custom-call | bytes 655360 | tf_op jit(solution)/shard_map/pallas_call | solution.py:554
  27.4 9.5 %collective-permute-done.2.refs_0_ = f32[5,64,256]{2,1,0:T(8,128)S(1)} collective-permute-done((f32[5,64,256]{2,1,0:T(8,128)S(1)}, f32[5,64,256]{2,1,0:T(8,128)S(1)}, u32[]{:S(2)}, u32[]{:S(2)}) %collective-permute-start.2) | collective-permute-done | bytes 327712 | tf_op jit(solution)/shard_map/ppermute | solution.py:534
  36.9 0.8 %shard_map.54.refs_1_ = f32[19,128,256]{2,1,0:T(8,128)} custom-call(f32[5,64,256]{2,1,0:T(8,128)S(1)} %collective-permute-done.2.refs_0_, f32[19,128,256]{2,1,0:T(8,128)} %shard_map.53.refs_1_), custom_call_target="tpu_custom_call", output_to_operand_aliasing={{}: (1, {})} | custom-call | bytes 655360 | tf_op jit(solution)/shard_map/pallas_call | solution.py:554
  37.7 0.0 collective-permute-done.5.refs_0_
  37.7 0.9 %shard_map.55.refs_2_ = f32[19,128,256]{2,1,0:T(8,128)} custom-call(f32[5,128,256]{2,1,0:T(8,128)S(1)} %collective-permute-done.5.refs_0_, f32[19,128,256]{2,1,0:T(8,128)} %shard_map.54.refs_1_), custom_call_target="tpu_custom_call", output_to_operand_aliasing={{}: (1, {})} | custom-call | bytes 655360 | tf_op jit(solution)/shard_map/pallas_call | solution.py:554
  38.6 2.6 %collective-permute-done.4.refs_1_ = f32[5,64,256]{2,1,0:T(8,128)S(1)} collective-permute-done((f32[5,64,256]{2,1,0:T(8,128)S(1)}, f32[5,64,256]{2,1,0:T(8,128)S(1)}, u32[]{:S(2)}, u32[]{:S(2)}) %collective-permute-start.4) | collective-permute-done | bytes 327712 | tf_op jit(solution)/shard_map/ppermute | solution.py:534
  41.2 0.8 %shard_map.56 = f32[19,128,256]{2,1,0:T(8,128)} custom-call(f32[5,64,256]{2,1,0:T(8,128)S(1)} %collective-permute-done.2.refs_0_, f32[5,64,256]{2,1,0:T(8,128)S(1)} %collective-permute-done.4.refs_1_, f32[19,128,256]{2,1,0:T(8,128)} %shard_map.55.refs_2_), custom_call_target="tpu_custom_call", output_to_operand_aliasing={{}: (2, {})} | custom-call | bytes 655360 | tf_op jit(solution)/shard_map/pallas_call | solution.py:554
  (1 shorter events, 0.0 us)
Async XLA Ops:
  2.9 15.7 %copy-start = (s32[1,128,256]{2,1,0:T(8,128)S(1)}, s32[1,128,256]{2,1,0:T(8,128)}, u32[]{:S(2)}) copy-start(s32[1,128,256]{2,1,0:T(8,128)} %param.5) | copy-start | bytes 393220
  3.0 15.7 %collective-permute-start.1 = (f32[5,128,256]{2,1,0:T(8,128)S(1)}, f32[5,128,256]{2,1,0:T(8,128)S(1)}, u32[]{:S(2)}, u32[]{:S(2)}) collective-permute-start(f32[5,128,256]{2,1,0:T(8,128)S(1)} %get-tuple-element.14), channel_id=1, source_target_pairs={{0,1},{1,0},{2,3},{3,2},{4,5},{5,4},{6,7},{7,6},{8,9},{9,8},{10,11... | collective-permute-start | bytes 1966088 | tf_op jit(solution)/shard_map/ppermute | solution.py:534
  5.0 13.7 %collective-permute-start = (f32[5,64,256]{2,1,0:T(8,128)S(1)}, f32[5,64,256]{2,1,0:T(8,128)S(1)}, u32[]{:S(2)}, u32[]{:S(2)}) collective-permute-start(f32[5,64,256]{2,1,0:T(8,128)S(1)} %get-tuple-element.13), channel_id=1, source_target_pairs={{0,15},{1,2},{2,1},{3,4},{4,3},{5,6},{6,5},{7,8},{8,7},{9,10},{10,... | collective-permute-start | bytes 983048 | tf_op jit(solution)/shard_map/ppermute | solution.py:534
  9.5 13.4 %collective-permute-start.3 = (f32[5,64,256]{2,1,0:T(8,128)S(1)}, f32[5,64,256]{2,1,0:T(8,128)S(1)}, u32[]{:S(2)}, u32[]{:S(2)}) collective-permute-start(f32[5,64,256]{2,1,0:T(8,128)S(1)} %shard_map.49), channel_id=1, source_target_pairs={{0,15},{1,2},{2,1},{3,4},{4,3},{5,6},{6,5},{7,8},{8,7},{9,10},{10,... | collective-permute-start | bytes 983048 | tf_op jit(solution)/shard_map/ppermute | solution.py:534
  23.6 14.1 %collective-permute-start.5 = (f32[5,128,256]{2,1,0:T(8,128)S(1)}, f32[5,128,256]{2,1,0:T(8,128)S(1)}, u32[]{:S(2)}, u32[]{:S(2)}) collective-permute-start(f32[5,128,256]{2,1,0:T(8,128)S(1)} %get-tuple-element.19), channel_id=1, source_target_pairs={{0,1},{1,0},{2,3},{3,2},{4,5},{5,4},{6,7},{7,6},{8,9},{9,8},{10,11... | collective-permute-start | bytes 1966088 | tf_op jit(solution)/shard_map/ppermute | solution.py:534
  24.1 12.8 %collective-permute-start.2 = (f32[5,64,256]{2,1,0:T(8,128)S(1)}, f32[5,64,256]{2,1,0:T(8,128)S(1)}, u32[]{:S(2)}, u32[]{:S(2)}) collective-permute-start(f32[5,64,256]{2,1,0:T(8,128)S(1)} %shard_map.48), channel_id=1, source_target_pairs={{0,15},{1,2},{2,1},{3,4},{4,3},{5,6},{6,5},{7,8},{8,7},{9,10},{10,... | collective-permute-start | bytes 983048 | tf_op jit(solution)/shard_map/ppermute | solution.py:534
  26.3 14.9 %collective-permute-start.4 = (f32[5,64,256]{2,1,0:T(8,128)S(1)}, f32[5,64,256]{2,1,0:T(8,128)S(1)}, u32[]{:S(2)}, u32[]{:S(2)}) collective-permute-start(f32[5,64,256]{2,1,0:T(8,128)S(1)} %shard_map.50), channel_id=1, source_target_pairs={{0,15},{1,2},{2,1},{3,4},{4,3},{5,6},{6,5},{7,8},{8,7},{9,10},{10,... | collective-permute-start | bytes 983048 | tf_op jit(solution)/shard_map/ppermute | solution.py:534
